TPU v7x, 32 devices: a whole 2x2x4 slice. The times are simulated.
32 devices in a mesh: row: 4 (over x, core), col: 8 (over z, y).
Axes of the slice: x: 2, y: 2, z: 4, core: 2. Of those that a mesh axis runs over, the one named last changes fastest.
Arguments:
- depth: float32 [3072, 8192], P('row', 'col'), may hold values from 0.05 to 2
- ground: float32 [3072, 8192], P('row', 'col'), may hold values from -4 to 4
- flow_rows: float32 [3072, 8192], P('row', 'col'), may hold values from -3 to 3
- flow_cols: float32 [3072, 8192], P('row', 'col'), may hold values from -3 to 3
- wet_tiles: int32 [4, 8], P('row', 'col'), may hold values 0 or 1
- inlet_cell: int32 [4, 8, 4096], P('row', 'col'), may hold values from 0 to 786431
- inlet_node: int32 [4, 8, 4096], P('row', 'col'), may hold values from 0 to 2047
- inlet_coef: float32 [4, 8, 4096], P('row', 'col'), may hold values from 0.05 to 0.5
- shift_rows: int32 [4, 8], P('row', 'col'), may hold values from 0 to 2, as said below
- shift_cols: int32 [4, 8], P('row', 'col'), may hold values from 0 to 2, as said below
Outputs:
- depth_out: float32 [3072, 8192], P('row', 'col')
- rows_out: float32 [3072, 8192], P('row', 'col')
- cols_out: float32 [3072, 8192], P('row', 'col')
- node_inflow: float32 [2048], P(('row', 'col'))
- moved_rows: float32 [3, 1024, 8192], P(None, 'row', 'col')
- moved_cols: float32 [3, 3072, 2048], P(None, 'row', 'col')
Inputs may be any that keep to these rules, and one draw needn't show every extreme that they name: `shift_rows`: some tile reaches 2 in every draw. `shift_cols`: some tile reaches 2 in every draw.
All inputs are finite; a program needn't handle non-finite values. No bound on the sum of `wet_tiles` on one device may be relied on, other than what follows from the above.
Results may differ from a plain program's by a relative error of at most 0.00002.
Values sent between devices are 32-bit elements; how exact they have to be, the bound alone decides.
A program may use at most 128 MiB of HBM per device.

v0:
```python
import jax
import jax.numpy as jnp
from jax import lax
from jax.sharding import PartitionSpec as P

STEPS = 3
BLOCK = 128
MAX_BLOCKS = 2
NODE_DEV = 64


gravity = 9.81
time_step = 0.1
friction = 0.0025
depth_floor = 0.25


def passed_along(value, axis, steps):
    count = lax.axis_size(axis)
    leading, last = (max(0, -steps), min(count, count - steps))
    return lax.ppermute(value, axis, [(source, source + steps) for source in range(leading, last)])


def face_update(flow, eta, eta_next, ground, ground_next):
    top = jnp.maximum(eta, eta_next) - jnp.maximum(ground, ground_next)
    face_depth = jnp.maximum(top, 0.0)
    floored = jnp.maximum(face_depth, depth_floor)
    pushed = flow - gravity * time_step * face_depth * (eta_next - eta)
    return pushed / (1.0 + gravity * time_step * friction * jnp.abs(flow) / floored ** (7.0 / 3.0))


def body(
    depth,
    ground,
    flow_rows,
    flow_cols,
    wet_tiles,
    inlet_cell,
    inlet_node,
    inlet_coef,
    shift_rows,
    shift_cols,
):
    tile_rows, tile_cols = depth.shape
    active = wet_tiles[0, 0] > 0
    for step in range(STEPS):
        eta = ground + depth
        next_row = passed_along(jnp.stack([eta[0], ground[0]]), "row", -1)
        next_col = passed_along(jnp.stack([eta[:, 0], ground[:, 0]]), "col", -1)
        eta_below = jnp.concatenate([eta[1:], next_row[0:1]], axis=0)
        ground_below = jnp.concatenate([ground[1:], next_row[1:2]], axis=0)
        eta_right = jnp.concatenate([eta[:, 1:], next_col[0][:, None]], axis=1)
        ground_right = jnp.concatenate([ground[:, 1:], next_col[1][:, None]], axis=1)
        cand_rows = face_update(flow_rows, eta, eta_below, ground, ground_below)
        cand_cols = face_update(flow_cols, eta, eta_right, ground, ground_right)
        new_rows = jnp.where(active, cand_rows, flow_rows)
        new_cols = jnp.where(active, cand_cols, flow_cols)
        prev_row = passed_along(new_rows[tile_rows - 1 :], "row", 1)
        prev_col = passed_along(new_cols[:, tile_cols - 1], "col", 1)
        before_rows = jnp.concatenate([prev_row, new_rows[:-1]], axis=0)
        before_cols = jnp.concatenate([prev_col[:, None], new_cols[:, :-1]], axis=1)
        new_depth = depth + time_step * (before_rows - new_rows + before_cols - new_cols)
        depth = jnp.where(active, new_depth, depth)
        flow_rows, flow_cols = (new_rows, new_cols)
    devices = lax.axis_size("row") * lax.axis_size("col")
    cells = inlet_cell[0, 0]
    captured = inlet_coef[0, 0] * jnp.maximum(depth.reshape(-1)[cells], 0.0)
    partial_value = jax.ops.segment_sum(captured, inlet_node[0, 0], num_segments=NODE_DEV * devices)
    node_inflow = lax.psum_scatter(partial_value, ("row", "col"), scatter_dimension=0, tiled=True)
    state = jnp.stack([depth, flow_rows, flow_cols])
    span = MAX_BLOCKS * BLOCK
    offsets = jnp.arange(span)
    mask_rows = offsets >= (MAX_BLOCKS - shift_rows[0, 0]) * BLOCK
    edge_rows = jnp.where(mask_rows[None, :, None], state[:, tile_rows - span :, :], 0.0)
    moved_rows = passed_along(edge_rows, "row", 1)
    mask_cols = offsets >= (MAX_BLOCKS - shift_cols[0, 0]) * BLOCK
    edge_cols = jnp.where(mask_cols[None, None, :], state[:, :, tile_cols - span :], 0.0)
    moved_cols = passed_along(edge_cols, "col", 1)
    return (depth, flow_rows, flow_cols, node_inflow, moved_rows, moved_cols)


def solution(mesh):
    return jax.shard_map(
        body,
        mesh=mesh,
        in_specs=(
            P("row", "col"),
            P("row", "col"),
            P("row", "col"),
            P("row", "col"),
            P("row", "col"),
            P("row", "col", None),
            P("row", "col", None),
            P("row", "col", None),
            P("row", "col"),
            P("row", "col"),
        ),
        out_specs=(
            P("row", "col"),
            P("row", "col"),
            P("row", "col"),
            P(("row", "col")),
            P(None, "row", "col"),
            P(None, "row", "col"),
        ),
        check_vma=False,
    )
```

profile of v0, /device:TPU:0, one launch (start us, length us, event | category | flops | bytes accessed | tf_op | source)
XLA Modules:
  0.0 231.4 jit_solution(8555999046566994930)
XLA Ops:
  0.6 1.2 slice_reduce_fusion.6
  1.8 3.9 %add.62 = f32[768,1024]{1,0:T(8,128)S(1)} add(f32[768,1024]{1,0:T(8,128)} %param.11, f32[768,1024]{1,0:T(8,128)} %param.10) | non-fusion elementwise | flops 786432 | bytes 9437184 | tf_op jit(solution)/shard_map/add | solution.py:47
  6.0 1.3 collective-permute-start.2
  8.0 1.3 collective-permute-start
  9.3 2.3 slice.178
  11.6 2.3 slice.138
  13.9 2.5 %slice.146 = f32[768,1023]{1,0:T(8,128)} slice(f32[768,1024]{1,0:T(8,128)S(1)} %copy-done), slice={[0:768], [1:1024]} | slice | bytes 6285312 | tf_op jit(solution)/shard_map/slice | solution.py:53
  16.4 2.5 %slice.184 = f32[768,1023]{1,0:T(8,128)} slice(f32[768,1024]{1,0:T(8,128)S(1)} %add.62), slice={[0:768], [1:1024]} | slice | bytes 6285312 | tf_op jit(solution)/shard_map/slice | solution.py:52
  19.8 0.9 copy.25
  20.7 0.8 fusion.28
  21.5 12.2 %divide_select_fusion.5 = (f32[768,1024]{1,0:T(8,128)S(1)}, f32[768,1024]{1,0:T(8,128)S(1)}) fusion(f32[768,1024]{1,0:T(8,128)} %param.12, f32[768,1024]{1,0:T(8,128)} %copy-done.5, f32[768,1024]{1,0:T(8,128)S(1)} %copy-done, f32[1,1024]{1,0:T(1,128)S(1)} %get-tuple-element.21, f32[1,1024]{1,0:T(1,128)S(1)} %get-tuple-element.20, f32[767,1024]{1,0:T(8,128)} %slice.178, ...), kind=kLoop, calls=%fused_computation.47 | loop fusion | flops 26738688 | bytes 31457280 | tf_op jit(solution)/shard_map/jit(_where)/select_n | solution.py:56
  33.8 3.0 %collective-permute-start.1 = (f32[1,1024]{1,0:T(1,128)S(1)}, f32[1,1024]{1,0:T(1,128)S(1)}, u32[]{:S(2)}, u32[]{:S(2)}) collective-permute-start(f32[1,1024]{1,0:T(1,128)S(1)} %slice.182), channel_id=1, source_target_pairs={{0,8},{8,16},{16,24},{1,9},{9,17},{17,25},{2,10},{10,18},{18,26},{... | collective-permute-start | bytes 12296 | tf_op jit(solution)/shard_map/ppermute | solution.py:21
  37.1 5.5 %collective-permute-start.3 = (f32[768]{0:T(1024)S(1)}, f32[768]{0:T(1024)S(1)}, u32[]{:S(2)}, u32[]{:S(2)}) collective-permute-start(f32[768]{0:T(1024)S(1)} %slice_reduce_fusion.4), channel_id=1, source_target_pairs={{0,1},{1,2},{2,3},{3,4},{4,5},{5,6},{6,7},{8,9},{9,10},{10,11},{11... | collective-permute-start | bytes 9224 | tf_op jit(solution)/shard_map/ppermute | solution.py:21
  42.6 1.3 collective-permute-done.3
  44.1 3.8 %fusion.25 = (f32[768,1024]{1,0:T(8,128)S(1)}, f32[768,1024]{1,0:T(8,128)}) fusion(f32[768,1024]{1,0:T(8,128)S(1)} %copy-done, f32[768,1024]{1,0:T(8,128)S(1)} %copy-done.13, f32[768,1024]{1,0:T(8,128)S(1)} %get-tuple-element.15, f32[768,1023]{1,0:T(8,128)S(1)} %bitcast.39, f32[768,1]{1,0:T(8,128)S(1)} %broadcast_in_dim.47, ...), kind=kLoop, calls=%fused_computation.78 | loop fusion | flops 7077888 | bytes 25165824 | tf_op jit(solution)/shard_map/add | solution.py:47
  48.1 1.3 collective-permute-start.6
  50.0 2.1 slice.190
  52.1 2.5 %slice.196 = f32[768,1023]{1,0:T(8,128)} slice(f32[768,1024]{1,0:T(8,128)S(1)} %get-tuple-element.8), slice={[0:768], [1:1024]} | slice | bytes 6285312 | tf_op jit(solution)/shard_map/slice | solution.py:52
  54.7 1.5 collective-permute-start.4
  56.3 0.9 copy.28
  57.3 1.0 collective-permute-done.4
  58.3 0.8 fusion.27
  59.1 12.2 %divide_select_fusion.3 = (f32[768,1024]{1,0:T(8,128)S(1)}, f32[768,1024]{1,0:T(8,128)S(1)}) fusion(f32[768,1024]{1,0:T(8,128)} %copy-done.9, f32[768,1024]{1,0:T(8,128)} %copy-done.4, f32[768,1024]{1,0:T(8,128)S(1)} %copy-done, f32[1,1024]{1,0:T(1,128)S(1)} %get-tuple-element.19, f32[1,1024]{1,0:T(1,128)S(1)} %get-tuple-element.18, f32[767,1024]{1,0:T(8,128)} %slice.190, ...), kind=kLoop, calls=%fused_computation.45 | loop fusion | flops 26738688 | bytes 31457280 | tf_op jit(solution)/shard_map/jit(_where)/select_n | solution.py:56
  71.4 4.5 %collective-permute-start.5 = (f32[1,1024]{1,0:T(1,128)S(1)}, f32[1,1024]{1,0:T(1,128)S(1)}, u32[]{:S(2)}, u32[]{:S(2)}) collective-permute-start(f32[1,1024]{1,0:T(1,128)S(1)} %slice.194), channel_id=1, source_target_pairs={{0,8},{8,16},{16,24},{1,9},{9,17},{17,25},{2,10},{10,18},{18,26},{... | collective-permute-start | bytes 12296 | tf_op jit(solution)/shard_map/ppermute | solution.py:21
  76.2 5.0 %collective-permute-start.7 = (f32[768]{0:T(1024)S(1)}, f32[768]{0:T(1024)S(1)}, u32[]{:S(2)}, u32[]{:S(2)}) collective-permute-start(f32[768]{0:T(1024)S(1)} %slice_reduce_fusion.2), channel_id=1, source_target_pairs={{0,1},{1,2},{2,3},{3,4},{4,5},{5,6},{6,7},{8,9},{9,10},{10,11},{11... | collective-permute-start | bytes 9224 | tf_op jit(solution)/shard_map/ppermute | solution.py:21
  82.6 3.8 %fusion.24 = (f32[768,1024]{1,0:T(8,128)S(1)}, f32[768,1024]{1,0:T(8,128)}) fusion(f32[768,1024]{1,0:T(8,128)S(1)} %copy-done, f32[768,1024]{1,0:T(8,128)S(1)} %copy-done.12, f32[768,1024]{1,0:T(8,128)S(1)} %get-tuple-element.13, f32[768,1023]{1,0:T(8,128)S(1)} %bitcast.38, f32[768,1]{1,0:T(8,128)S(1)} %broadcast_in_dim.48, ...), kind=kLoop, calls=%fused_computation.77 | loop fusion | flops 7077888 | bytes 25165824 | tf_op jit(solution)/shard_map/add | solution.py:47
  86.7 1.3 collective-permute-start.10
  88.0 2.1 slice.202
  90.1 2.5 %slice.208 = f32[768,1023]{1,0:T(8,128)} slice(f32[768,1024]{1,0:T(8,128)S(1)} %get-tuple-element.6), slice={[0:768], [1:1024]} | slice | bytes 6285312 | tf_op jit(solution)/shard_map/slice | solution.py:52
  92.6 1.3 collective-permute-start.8
  94.1 0.9 copy.31
  95.0 0.7 collective-permute-done.8
  95.8 0.8 fusion.26
  96.6 12.2 %divide_select_fusion.1 = (f32[768,1024]{1,0:T(8,128)S(1)}, f32[768,1024]{1,0:T(8,128)S(1)}) fusion(f32[768,1024]{1,0:T(8,128)} %copy-done.8, f32[768,1024]{1,0:T(8,128)} %copy-done.3, f32[768,1024]{1,0:T(8,128)S(1)} %copy-done, f32[1,1024]{1,0:T(1,128)S(1)} %get-tuple-element.17, f32[1,1024]{1,0:T(1,128)S(1)} %get-tuple-element.16, f32[767,1024]{1,0:T(8,128)} %slice.202, ...), kind=kLoop, calls=%fused_computation.43 | loop fusion | flops 26738688 | bytes 31457280 | tf_op jit(solution)/shard_map/jit(_where)/select_n | solution.py:56
  108.8 2.9 %collective-permute-start.9 = (f32[1,1024]{1,0:T(1,128)S(1)}, f32[1,1024]{1,0:T(1,128)S(1)}, u32[]{:S(2)}, u32[]{:S(2)}) collective-permute-start(f32[1,1024]{1,0:T(1,128)S(1)} %slice.206), channel_id=1, source_target_pairs={{0,8},{8,16},{16,24},{1,9},{9,17},{17,25},{2,10},{10,18},{18,26},{... | collective-permute-start | bytes 12296 | tf_op jit(solution)/shard_map/ppermute | solution.py:21
  112.1 5.9 %collective-permute-start.11 = (f32[768]{0:T(1024)S(1)}, f32[768]{0:T(1024)S(1)}, u32[]{:S(2)}, u32[]{:S(2)}) collective-permute-start(f32[768]{0:T(1024)S(1)} %slice_reduce_fusion), channel_id=1, source_target_pairs={{0,1},{1,2},{2,3},{3,4},{4,5},{5,6},{6,7},{8,9},{9,10},{10,11},{11... | collective-permute-start | bytes 9224 | tf_op jit(solution)/shard_map/ppermute | solution.py:21
  118.1 1.1 collective-permute-done.11
  119.3 2.0 add_select_fusion
  121.3 2.4 %maximum_select_fusion = f32[3,256,1024]{2,1,0:T(8,128)} fusion(f32[1,768,1024]{2,1,0:T(8,128)S(1)} %bitcast.33, f32[1,768,1024]{2,1,0:T(8,128)S(1)} %bitcast.36, f32[1,768,1024]{2,1,0:T(8,128)S(1)} %bitcast.42, pred[256]{0:T(512)(128)(4,1)S(1)} %iota_compare_fusion.1), kind=kLoop, calls=%fused_computation.5 | loop fusion | flops 2359296 | bytes 12583168 | tf_op jit(solution)/shard_map/jit(_where)/select_n | solution.py:74
  123.7 2.9 %collective-permute-start.12 = (f32[3,256,1024]{2,1,0:T(8,128)}, f32[3,256,1024]{2,1,0:T(8,128)}, u32[]{:S(2)}, u32[]{:S(2)}) collective-permute-start(f32[3,256,1024]{2,1,0:T(8,128)} %maximum_select_fusion), channel_id=1, source_target_pairs={{0,8},{8,16},{16,24},{1,9},{9,17},{17,25},{2,10},{10,18},{18,26},{... | collective-permute-start | bytes 9437192 | tf_op jit(solution)/shard_map/ppermute | solution.py:21
  127.4 1.7 fusion.21
  129.1 6.3 %collective-permute-start.13 = (f32[3,768,256]{2,1,0:T(8,128)}, f32[3,768,256]{2,1,0:T(8,128)}, u32[]{:S(2)}, u32[]{:S(2)}) collective-permute-start(f32[3,768,256]{2,1,0:T(8,128)} %fusion.21), channel_id=1, source_target_pairs={{0,1},{1,2},{2,3},{3,4},{4,5},{5,6},{6,7},{8,9},{9,10},{10,11},{11... | collective-permute-start | bytes 7077896 | tf_op jit(solution)/shard_map/ppermute | solution.py:21
  135.4 2.6 %copy.34 = f32[96,8,8,128]{3,1,2,0:T(8,128)S(1)} copy(f32[96,8,8,128]{3,2,1,0:T(8,128)} %bitcast.44) | data formatting | bytes 6291456
  138.0 23.0 %gather_fusion = f32[4096]{0:T(1024)S(1)} fusion(f32[786432]{0:T(1024)S(1)} %bitcast.31, s32[4096]{0:T(1024)S(1)} %broadcast_clamp_fusion), kind=kCustom, calls=%fused_computation | custom fusion | bytes 49152 | tf_op jit(solution)/shard_map/gather | solution.py:67
  161.1 22.2 %scatter_custom_fusion = f32[2048]{0:T(1024)S(1)} fusion(s32[4096]{0:T(1024)} %bitcast.47, f32[4096]{0:T(1024)S(1)} %maximum_multiply_fusion, f32[]{:T(128)} %constant.13.clone.1), kind=kCustom, calls=%fused_computation.67 | custom fusion | flops 4096 | bytes 8704 | tf_op jit(solution)/shard_map/scatter-add | solution.py:68
  183.3 40.4 %all-reduce = f32[2048]{0:T(1024)S(1)} all-reduce(f32[2048]{0:T(1024)S(1)} %scatter_custom_fusion), channel_id=2, replica_groups=mesh['row'=4,'col'=8] {'row','col'}, use_global_device_ids=true, to_apply=%region_1.2.clone | all-reduce | flops 2048 | bytes 16384
  224.2 4.0 %copy.40 = f32[3,256,1024]{2,1,0:T(8,128)} copy(f32[3,256,1024]{2,1,0:T(8,128)} %collective-permute-done.12) | data formatting | bytes 6291456
  228.2 3.2 %copy.41 = f32[3,768,256]{2,1,0:T(8,128)} copy(f32[3,768,256]{2,1,0:T(8,128)} %collective-permute-done.13) | data formatting | bytes 4718592
  (80 shorter events, 5.2 us)
Async XLA Ops:
  1.8 5.5 %copy-start = (f32[768,1024]{1,0:T(8,128)S(1)}, f32[768,1024]{1,0:T(8,128)}, u32[]{:S(2)}) copy-start(f32[768,1024]{1,0:T(8,128)} %param.11) | copy-start | bytes 9437188
  5.8 10.6 %copy-start.5 = (f32[768,1024]{1,0:T(8,128)}, f32[768,1024]{1,0:T(8,128)S(1)}, u32[]{:S(2)}) copy-start(f32[768,1024]{1,0:T(8,128)S(1)} %add.62) | copy-start | bytes 9437188
  6.0 13.6 %collective-permute-start.2 = (f32[2,768]{1,0:T(2,128)S(1)}, f32[2,768]{1,0:T(2,128)S(1)}, u32[]{:S(2)}, u32[]{:S(2)}) collective-permute-start(f32[2,768]{1,0:T(2,128)S(1)} %pad_maximum_fusion.13), channel_id=1, source_target_pairs={{1,0},{2,1},{3,2},{4,3},{5,4},{6,5},{7,6},{9,8},{10,9},{11,10},{12... | collective-permute-start | bytes 18440 | tf_op jit(solution)/shard_map/ppermute | solution.py:21
  8.0 12.8 %collective-permute-start = (f32[2,1024]{1,0:T(2,128)}, f32[2,1024]{1,0:T(2,128)}, u32[]{:S(2)}, u32[]{:S(2)}) collective-permute-start(f32[2,1024]{1,0:T(2,128)} %pad_maximum_fusion.10), channel_id=1, source_target_pairs={{8,0},{16,8},{24,16},{9,1},{17,9},{25,17},{10,2},{18,10},{26,18},{... | collective-permute-start | bytes 24584 | tf_op jit(solution)/shard_map/ppermute | solution.py:21
  21.5 22.6 %copy-start.13 = (f32[768,1024]{1,0:T(8,128)S(1)}, f32[768,1024]{1,0:T(8,128)}, u32[]{:S(2)}) copy-start(f32[768,1024]{1,0:T(8,128)} %param.10) | copy-start | bytes 9437188
  33.7 14.2 %copy-start.7 = (f32[768,1024]{1,0:T(8,128)}, f32[768,1024]{1,0:T(8,128)S(1)}, u32[]{:S(2)}) copy-start(f32[768,1024]{1,0:T(8,128)S(1)} %get-tuple-element.15) | copy-start | bytes 9437188
  33.7 14.2 %copy-start.9 = (f32[768,1024]{1,0:T(8,128)}, f32[768,1024]{1,0:T(8,128)S(1)}, u32[]{:S(2)}) copy-start(f32[768,1024]{1,0:T(8,128)S(1)} %get-tuple-element.14) | copy-start | bytes 9437188
  33.8 10.3 %collective-permute-start.1 = (f32[1,1024]{1,0:T(1,128)S(1)}, f32[1,1024]{1,0:T(1,128)S(1)}, u32[]{:S(2)}, u32[]{:S(2)}) collective-permute-start(f32[1,1024]{1,0:T(1,128)S(1)} %slice.182), channel_id=1, source_target_pairs={{0,8},{8,16},{16,24},{1,9},{9,17},{17,25},{2,10},{10,18},{18,26},{... | collective-permute-start | bytes 12296 | tf_op jit(solution)/shard_map/ppermute | solution.py:21
  37.1 6.8 %collective-permute-start.3 = (f32[768]{0:T(1024)S(1)}, f32[768]{0:T(1024)S(1)}, u32[]{:S(2)}, u32[]{:S(2)}) collective-permute-start(f32[768]{0:T(1024)S(1)} %slice_reduce_fusion.4), channel_id=1, source_target_pairs={{0,1},{1,2},{2,3},{3,4},{4,5},{5,6},{6,7},{8,9},{9,10},{10,11},{11... | collective-permute-start | bytes 9224 | tf_op jit(solution)/shard_map/ppermute | solution.py:21
  47.9 4.2 %copy-start.4 = (f32[768,1024]{1,0:T(8,128)}, f32[768,1024]{1,0:T(8,128)S(1)}, u32[]{:S(2)}) copy-start(f32[768,1024]{1,0:T(8,128)S(1)} %get-tuple-element.8) | copy-start | bytes 9437188
  48.1 8.0 %collective-permute-start.6 = (f32[2,768]{1,0:T(2,128)S(1)}, f32[2,768]{1,0:T(2,128)S(1)}, u32[]{:S(2)}, u32[]{:S(2)}) collective-permute-start(f32[2,768]{1,0:T(2,128)S(1)} %pad_maximum_fusion.12), channel_id=1, source_target_pairs={{1,0},{2,1},{3,2},{4,3},{5,4},{6,5},{7,6},{9,8},{10,9},{11,10},{12... | collective-permute-start | bytes 18440 | tf_op jit(solution)/shard_map/ppermute | solution.py:21
  54.7 3.7 %collective-permute-start.4 = (f32[2,1024]{1,0:T(2,128)}, f32[2,1024]{1,0:T(2,128)}, u32[]{:S(2)}, u32[]{:S(2)}) collective-permute-start(f32[2,1024]{1,0:T(2,128)} %pad_maximum_fusion.9), channel_id=1, source_target_pairs={{8,0},{16,8},{24,16},{9,1},{17,9},{25,17},{10,2},{18,10},{26,18},{... | collective-permute-start | bytes 24584 | tf_op jit(solution)/shard_map/ppermute | solution.py:21
  59.1 23.5 %copy-start.12 = (f32[768,1024]{1,0:T(8,128)S(1)}, f32[768,1024]{1,0:T(8,128)}, u32[]{:S(2)}) copy-start(f32[768,1024]{1,0:T(8,128)} %get-tuple-element.9) | copy-start | bytes 9437188
  71.3 15.1 %copy-start.6 = (f32[768,1024]{1,0:T(8,128)}, f32[768,1024]{1,0:T(8,128)S(1)}, u32[]{:S(2)}) copy-start(f32[768,1024]{1,0:T(8,128)S(1)} %get-tuple-element.13) | copy-start | bytes 9437188
  71.3 15.1 %copy-start.8 = (f32[768,1024]{1,0:T(8,128)}, f32[768,1024]{1,0:T(8,128)S(1)}, u32[]{:S(2)}) copy-start(f32[768,1024]{1,0:T(8,128)S(1)} %get-tuple-element.12) | copy-start | bytes 9437188
  71.4 11.2 %collective-permute-start.5 = (f32[1,1024]{1,0:T(1,128)S(1)}, f32[1,1024]{1,0:T(1,128)S(1)}, u32[]{:S(2)}, u32[]{:S(2)}) collective-permute-start(f32[1,1024]{1,0:T(1,128)S(1)} %slice.194), channel_id=1, source_target_pairs={{0,8},{8,16},{16,24},{1,9},{9,17},{17,25},{2,10},{10,18},{18,26},{... | collective-permute-start | bytes 12296 | tf_op jit(solution)/shard_map/ppermute | solution.py:21
  76.2 6.3 %collective-permute-start.7 = (f32[768]{0:T(1024)S(1)}, f32[768]{0:T(1024)S(1)}, u32[]{:S(2)}, u32[]{:S(2)}) collective-permute-start(f32[768]{0:T(1024)S(1)} %slice_reduce_fusion.2), channel_id=1, source_target_pairs={{0,1},{1,2},{2,3},{3,4},{4,5},{5,6},{6,7},{8,9},{9,10},{10,11},{11... | collective-permute-start | bytes 9224 | tf_op jit(solution)/shard_map/ppermute | solution.py:21
  86.4 3.6 %copy-start.3 = (f32[768,1024]{1,0:T(8,128)}, f32[768,1024]{1,0:T(8,128)S(1)}, u32[]{:S(2)}) copy-start(f32[768,1024]{1,0:T(8,128)S(1)} %get-tuple-element.6) | copy-start | bytes 9437188
  86.7 7.2 %collective-permute-start.10 = (f32[2,768]{1,0:T(2,128)S(1)}, f32[2,768]{1,0:T(2,128)S(1)}, u32[]{:S(2)}, u32[]{:S(2)}) collective-permute-start(f32[2,768]{1,0:T(2,128)S(1)} %pad_maximum_fusion.11), channel_id=1, source_target_pairs={{1,0},{2,1},{3,2},{4,3},{5,4},{6,5},{7,6},{9,8},{10,9},{11,10},{12... | collective-permute-start | bytes 18440 | tf_op jit(solution)/shard_map/ppermute | solution.py:21
  92.6 3.2 %collective-permute-start.8 = (f32[2,1024]{1,0:T(2,128)S(1)}, f32[2,1024]{1,0:T(2,128)}, u32[]{:S(2)}, u32[]{:S(2)}) collective-permute-start(f32[2,1024]{1,0:T(2,128)S(1)} %pad_maximum_fusion.8), channel_id=1, source_target_pairs={{8,0},{16,8},{24,16},{9,1},{17,9},{25,17},{10,2},{18,10},{26,18},{... | collective-permute-start | bytes 24584 | tf_op jit(solution)/shard_map/ppermute | solution.py:21
  96.6 22.8 %copy-start.11 = (f32[768,1024]{1,0:T(8,128)S(1)}, f32[768,1024]{1,0:T(8,128)}, u32[]{:S(2)}) copy-start(f32[768,1024]{1,0:T(8,128)} %get-tuple-element.7) | copy-start | bytes 9437188
  108.8 18.5 %copy-start.1 = (f32[768,1024]{1,0:T(8,128)}, f32[768,1024]{1,0:T(8,128)S(1)}, u32[]{:S(2)}) copy-start(f32[768,1024]{1,0:T(8,128)S(1)} %get-tuple-element.36) | copy-start | bytes 9437188
  108.8 18.5 %copy-start.2 = (f32[768,1024]{1,0:T(8,128)}, f32[768,1024]{1,0:T(8,128)S(1)}, u32[]{:S(2)}) copy-start(f32[768,1024]{1,0:T(8,128)S(1)} %get-tuple-element.35) | copy-start | bytes 9437188
  108.8 10.5 %collective-permute-start.9 = (f32[1,1024]{1,0:T(1,128)S(1)}, f32[1,1024]{1,0:T(1,128)S(1)}, u32[]{:S(2)}, u32[]{:S(2)}) collective-permute-start(f32[1,1024]{1,0:T(1,128)S(1)} %slice.206), channel_id=1, source_target_pairs={{0,8},{8,16},{16,24},{1,9},{9,17},{17,25},{2,10},{10,18},{18,26},{... | collective-permute-start | bytes 12296 | tf_op jit(solution)/shard_map/ppermute | solution.py:21
  112.1 7.0 %collective-permute-start.11 = (f32[768]{0:T(1024)S(1)}, f32[768]{0:T(1024)S(1)}, u32[]{:S(2)}, u32[]{:S(2)}) collective-permute-start(f32[768]{0:T(1024)S(1)} %slice_reduce_fusion), channel_id=1, source_target_pairs={{0,1},{1,2},{2,3},{3,4},{4,5},{5,6},{6,7},{8,9},{9,10},{10,11},{11... | collective-permute-start | bytes 9224 | tf_op jit(solution)/shard_map/ppermute | solution.py:21
  121.3 6.0 %copy-start.10 = (f32[768,1024]{1,0:T(8,128)}, f32[768,1024]{1,0:T(8,128)S(1)}, u32[]{:S(2)}) copy-start(f32[768,1024]{1,0:T(8,128)S(1)} %add_select_fusion) | copy-start | bytes 9437188
  123.7 100.5 %collective-permute-start.12 = (f32[3,256,1024]{2,1,0:T(8,128)}, f32[3,256,1024]{2,1,0:T(8,128)}, u32[]{:S(2)}, u32[]{:S(2)}) collective-permute-start(f32[3,256,1024]{2,1,0:T(8,128)} %maximum_select_fusion), channel_id=1, source_target_pairs={{0,8},{8,16},{16,24},{1,9},{9,17},{17,25},{2,10},{10,18},{18,26},{... | collective-permute-start | bytes 9437192 | tf_op jit(solution)/shard_map/ppermute | solution.py:21
  127.4 8.0 %copy-start.15 = (s32[1,1,4096]{2,1,0:T(1,128)S(1)}, s32[1,1,4096]{2,1,0:T(1,128)}, u32[]{:S(2)}) copy-start(s32[1,1,4096]{2,1,0:T(1,128)} %param.15) | copy-start | bytes 49156
  129.1 95.2 %collective-permute-start.13 = (f32[3,768,256]{2,1,0:T(8,128)}, f32[3,768,256]{2,1,0:T(8,128)}, u32[]{:S(2)}, u32[]{:S(2)}) collective-permute-start(f32[3,768,256]{2,1,0:T(8,128)} %fusion.21), channel_id=1, source_target_pairs={{0,1},{1,2},{2,3},{3,4},{4,5},{5,6},{6,7},{8,9},{9,10},{10,11},{11... | collective-permute-start | bytes 7077896 | tf_op jit(solution)/shard_map/ppermute | solution.py:21
  138.0 23.1 %copy-start.14 = (f32[1,1,4096]{2,1,0:T(1,128)S(1)}, f32[1,1,4096]{2,1,0:T(1,128)}, u32[]{:S(2)}) copy-start(f32[1,1,4096]{2,1,0:T(1,128)} %param.17) | copy-start | bytes 49156
where the time goes:
time: 232 us; the launch traced here: 231 us
  other arithmetic  77.7 us (33%)
  local copies, waits for them, and re-layouts  61.3 us (26%)
  starting transfers between devices  43.9 us (19%)
  blocking collectives  40.4 us (17%)
  waiting for transfers between devices  4.84 us (2%)
  between operations  3.23 us (1%)
    ppermute x14, starting transfers between devices, passed_along(): lax.ppermute(value, axis, [(source, source + steps) for source in range(l...  43.9 us
    unnamed x1, blocking collectives  40.4 us
    select_n x3, other arithmetic, body(): new_rows = jnp.where(active, cand_rows, flow_rows)  36.6 us
    gather x1, local copies, waits for them, and re-layouts, body(): captured = inlet_coef[0, 0] * jnp.maximum(depth.reshape(-1)[cells], 0.0)  23 us
    scatter-add x1, other arithmetic, body(): jax.ops.segment_sum(captured, inlet_node[0, 0], num_segments=NODE_DEV * d...  22.2 us
    add x3, other arithmetic, body(): eta = ground + depth  11.5 us
    unnamed x36, local copies, waits for them, and re-layouts  10.5 us
    slice x6, local copies, waits for them, and re-layouts, body(): eta_below = jnp.concatenate([eta[1:], next_row[0:1]], axis=0)  8.8 us
  transfers between devices with their start and end apart: 14, of which 5 were waited for; matrix products, arithmetic and copies ran while one was open for 32% of the time, Pallas kernels for 0%

commit v1 on v0

v1 whole, which is shorter than its diff:
```python
import functools

import jax
import jax.numpy as jnp
from jax import lax
from jax.experimental import pallas as pl
from jax.experimental.pallas import tpu as pltpu
from jax.sharding import PartitionSpec as P

STEPS = 3
BLOCK = 128
MAX_BLOCKS = 2
NODE_DEV = 64
LANES = 128
SUB = 8
EDGE = 4


gravity = 9.81
time_step = 0.1
friction = 0.0025
depth_floor = 0.25


def passed_along(value, axis, steps):
    count = lax.axis_size(axis)
    leading, last = (max(0, -steps), min(count, count - steps))
    return lax.ppermute(value, axis, [(source, source + steps) for source in range(leading, last)])


def face_update(flow, eta, eta_next, top_ground):
    face_depth = jnp.maximum(jnp.maximum(eta, eta_next) - top_ground, 0.0)
    floored = jnp.maximum(face_depth, depth_floor)
    drag = (gravity * time_step * friction) * jnp.abs(flow) * jnp.exp((-7.0 / 3.0) * jnp.log(floored))
    pushed = flow - (gravity * time_step) * face_depth * (eta_next - eta)
    return pushed / (1.0 + drag)


def steps_kernel(cs, row0, rows, kind, *refs):
    depth, ground, frow, fcol, top, bottom, side, wet, shift = refs[:9]
    if kind == "all":
        outs, scratch = refs[9:12], refs[12:]
    else:
        outs, scratch = refs[9:10], refs[10:]
    d, g, f, c, w8, zc, zero, in_sem, side_sem, out_sem = scratch
    n = len(cs)
    high = rows - row0 + 32
    arrays = ((depth, d), (ground, g), (frow, f), (fcol, c))
    copies = []
    for a, (src, dst) in enumerate(arrays):
        for i, slab in enumerate(cs[:-1]):
            copies.append(pltpu.make_async_copy(
                src.at[pl.ds(row0, rows - row0), pl.ds(slab * LANES, LANES)],
                dst.at[pl.ds(i * high + 16, rows - row0)], in_sem.at[a, i]))
    skip = 0 if row0 == 0 else 16
    for a, dst in enumerate((d, g, f, c, w8)):
        base = (n - 1) * high if a < 4 else 0
        copies.append(pltpu.make_async_copy(
            side.at[a, pl.ds(row0 + skip, high - skip)], dst.at[pl.ds(base + skip, high - skip)], side_sem.at[a]))
    for copy in copies:
        copy.start()
    blank = jnp.zeros((SUB, LANES), jnp.float32)
    for a, (_, dst) in enumerate(arrays):
        for i in range(n):
            if i == n - 1 and row0 == 0:
                continue
            dst[pl.ds(i * high, SUB), :] = blank
            if i == n - 1:
                dst[pl.ds(i * high + 8, SUB), :] = blank
                continue
            lanes = pl.ds(cs[i] * LANES, LANES)
            dst[pl.ds(i * high + 8, SUB), :] = top[a, :, lanes] if row0 == 0 else blank
            dst[pl.ds(i * high + high - 16, SUB), :] = bottom[a, :, lanes]
            dst[pl.ds(i * high + high - 8, SUB), :] = blank
    if kind != "all":
        zero[...] = jnp.zeros_like(zero)
    for copy in copies:
        copy.wait()

    lane = lax.broadcasted_iota(jnp.int32, (SUB, LANES), 1)
    at_last, at_first = lane == LANES - 1, lane == 0

    def rightward(vals):
        rolled = [pltpu.roll(v, LANES - 1, 1) for v in vals]
        return [jnp.where(at_last, rolled[(i + 1) % n], rolled[i]) for i in range(n)]

    def leftward(vals):
        rolled = [pltpu.roll(v, 1, 1) for v in vals]
        return [jnp.where(at_first, rolled[(i - 1) % n], rolled[i]) for i in range(n)]

    first = 1 if row0 == 0 else 2
    last = high // SUB - 2
    sizes = [i * high for i in range(n)]

    def bed(b, carry):
        r = pl.multiple_of(b * SUB, SUB)
        vals = [g[pl.ds(s + r, SUB), :] for s in sizes]
        for s, v, q in zip(sizes, vals, rightward(vals)):
            zc[pl.ds(s + r, SUB), :] = jnp.maximum(v, q)
        return carry

    lax.fori_loop(first, last + 1, bed, 0)
    active = jnp.broadcast_to(wet[0, 0], (SUB, LANES)) > 0
    top_active = top[4, :, pl.ds(0, LANES)] > 0.0
    bottom_active = bottom[4, :, pl.ds(0, LANES)] > 0.0

    def block(b, mask):
        r = b * SUB if isinstance(b, int) else pl.multiple_of(b * SUB, SUB)
        masks = [mask] * (n - 1) + [w8[pl.ds(r, SUB), :] > 0.0]
        depths = [d[pl.ds(s + r, SUB), :] for s in sizes]
        grounds = [g[pl.ds(s + r, SUB), :] for s in sizes]
        eta = [x + y for x, y in zip(depths, grounds)]
        right = rightward(eta)
        cols = []
        for i, s in enumerate(sizes):
            old = c[pl.ds(s + r, SUB), :]
            new = face_update(old, eta[i], right[i], zc[pl.ds(s + r, SUB), :])
            new = jnp.where(masks[i], new, old)
            c[pl.ds(s + r, SUB), :] = new
            cols.append(new)
        before = leftward(cols)
        for i, s in enumerate(sizes):
            below = g[pl.ds(s + r + 1, SUB), :]
            old = f[pl.ds(s + r, SUB), :]
            eta_below = d[pl.ds(s + r + 1, SUB), :] + below
            new = face_update(old, eta[i], eta_below, jnp.maximum(grounds[i], below))
            new = jnp.where(masks[i], new, old)
            f[pl.ds(s + r, SUB), :] = new
            above = f[pl.ds(s + r - 1, SUB), :]
            moved = depths[i] + time_step * (above - new + before[i] - cols[i])
            d[pl.ds(s + r, SUB), :] = jnp.where(masks[i], moved, depths[i])

    def inner(b, carry):
        block(b, active)
        return carry

    for _ in range(STEPS):
        if row0 == 0:
            block(1, top_active)
        lax.fori_loop(2, last, inner, 0)
        block(last, bottom_active)

    span = MAX_BLOCKS * BLOCK
    state = (d, f, c)
    copies = []
    for a, src in enumerate(state):
        if kind == "all":
            for i, slab in enumerate(cs[:-1]):
                copies.append(pltpu.make_async_copy(
                    src.at[pl.ds(i * high + 16, rows)], outs[a].at[:, pl.ds(slab * LANES, LANES)], out_sem.at[a, i]))
                copies[-1].start()
            continue
        for k in range(MAX_BLOCKS):
            keep = k >= MAX_BLOCKS - shift[0, 0]
            if kind == "cols":
                pieces = [(src.at[pl.ds((n - 1 - MAX_BLOCKS + k) * high + 16, rows)], zero,
                           outs[0].at[a, :, pl.ds(k * BLOCK, BLOCK)], k)]
            else:
                pieces = [(src.at[pl.ds(i * high + high - 16 - span + k * BLOCK, BLOCK)], zero,
                           outs[0].at[a, pl.ds(k * BLOCK, BLOCK), pl.ds(slab * LANES, LANES)], k * n + i)
                          for i, slab in enumerate(cs[:-1])]
            for data, empty, dst, m in pieces:
                copy = pltpu.make_async_copy(data, dst, out_sem.at[a, m])
                hole = pltpu.make_async_copy(empty, dst, out_sem.at[a, m])
                pl.when(keep)(copy.start)
                pl.when(jnp.logical_not(keep))(hole.start)
                copies.append(copy)
    for copy in copies:
        copy.wait()


def steps_call(kind, args):
    rows, width = args[0].shape
    slabs = width // LANES
    cs, row0 = list(range(slabs + 1)), 0
    span = MAX_BLOCKS * BLOCK
    if kind == "cols":
        cs = cs[slabs - MAX_BLOCKS - 1:]
        out = [jax.ShapeDtypeStruct((3, rows, span), jnp.float32)]
        zero, sems = (rows, LANES), MAX_BLOCKS
    elif kind == "rows":
        row0 = rows - span - SUB
        out = [jax.ShapeDtypeStruct((3, span, width), jnp.float32)]
        zero, sems = (BLOCK, LANES), MAX_BLOCKS * len(cs)
    else:
        out = [jax.ShapeDtypeStruct((rows, width), jnp.float32)] * 3
        zero, sems = (SUB, LANES), len(cs)
    n, high = len(cs), rows - row0 + 32
    anywhere = pl.BlockSpec(memory_space=pl.ANY)
    vmem = pl.BlockSpec(memory_space=pltpu.VMEM)
    smem = pl.BlockSpec(memory_space=pltpu.SMEM)
    buffer = pltpu.VMEM((n * high, LANES), jnp.float32)
    cells = n * high * LANES
    return pl.pallas_call(
        functools.partial(steps_kernel, cs, row0, rows, kind),
        out_shape=out,
        in_specs=[anywhere] * 4 + [vmem, vmem, anywhere, smem, smem],
        out_specs=[anywhere] * len(out),
        scratch_shapes=[buffer] * 4 + [pltpu.VMEM((high, LANES), jnp.float32), buffer, pltpu.VMEM(zero, jnp.float32),
                                       pltpu.SemaphoreType.DMA((4, n)), pltpu.SemaphoreType.DMA((5,)),
                                       pltpu.SemaphoreType.DMA((3, sems))],
        compiler_params=pltpu.CompilerParams(vmem_limit_bytes=40 << 20),
        cost_estimate=pl.CostEstimate(flops=200 * cells, transcendentals=18 * cells, bytes_accessed=28 * cells),
        name="steps_" + kind,
    )(*args)


def pick_kernel(spots, depth, out, slabs, sem):
    rows, width = depth.shape
    copies = [pltpu.make_async_copy(depth.at[:, pl.ds(i * LANES, LANES)], slabs.at[pl.ds(i * rows, rows)], sem.at[i])
              for i in range(width // LANES)]
    for copy in copies:
        copy.start()
    for copy in copies:
        copy.wait()

    def body(k, carry):
        base = pl.multiple_of(k * 16, 16)
        for j in range(16):
            out[pl.ds(base + j, 1), :] = slabs[pl.ds(spots[base + j], 1), :]
        return carry

    lax.fori_loop(0, out.shape[0] // 16, body, 0)


def pick_rows(spots, depth):
    rows, width = depth.shape
    count = spots.shape[0]
    return pl.pallas_call(
        pick_kernel,
        out_shape=jax.ShapeDtypeStruct((count, LANES), jnp.float32),
        in_specs=[pl.BlockSpec(memory_space=pltpu.SMEM), pl.BlockSpec(memory_space=pl.ANY)],
        out_specs=pl.BlockSpec(memory_space=pltpu.VMEM),
        scratch_shapes=[pltpu.VMEM((rows * width // LANES, LANES), jnp.float32),
                        pltpu.SemaphoreType.DMA((width // LANES,))],
        compiler_params=pltpu.CompilerParams(vmem_limit_bytes=16 << 20),
        cost_estimate=pl.CostEstimate(flops=0, transcendentals=0, bytes_accessed=8 * rows * width),
        name="pick_rows",
    )(spots, depth)


def halos(arrays, wet):
    rows, width = arrays[0].shape
    flag = wet.astype(jnp.float32)
    full = lambda shape: jnp.broadcast_to(flag, shape)
    first = jnp.stack([x[:SUB] for x in arrays] + [full((SUB, width))])
    last = jnp.stack([x[rows - SUB:] for x in arrays] + [full((SUB, width))])
    top = passed_along(last, "row", 1)
    bottom = passed_along(first, "row", -1)

    def columns(start):
        mid = jnp.stack([x[:, start:start + EDGE].T for x in arrays] + [full((EDGE, rows))])
        ends = [jnp.swapaxes(x[:, :, start:start + EDGE], 1, 2) for x in (top, bottom)]
        return jnp.concatenate([ends[0], mid, ends[1]], axis=2)

    left = passed_along(columns(width - EDGE), "col", 1)
    right = passed_along(columns(0), "col", -1)
    gap = jnp.zeros((5, LANES - 2 * EDGE, rows + 2 * SUB), jnp.float32)
    side = jnp.swapaxes(jnp.concatenate([right, gap, left], axis=1), 1, 2)
    return top, bottom, jnp.pad(side, ((0, 0), (SUB, SUB), (0, 0)))


def body(
    depth,
    ground,
    flow_rows,
    flow_cols,
    wet_tiles,
    inlet_cell,
    inlet_node,
    inlet_coef,
    shift_rows,
    shift_cols,
):
    tile_rows, tile_cols = depth.shape
    arrays = (depth, ground, flow_rows, flow_cols)
    top, bottom, side = halos(arrays, wet_tiles[0, 0])
    common = arrays + (top, bottom, side, wet_tiles)
    (edge_cols,) = steps_call("cols", common + (shift_cols,))
    moved_cols = passed_along(edge_cols, "col", 1)
    (edge_rows,) = steps_call("rows", common + (shift_rows,))
    moved_rows = passed_along(edge_rows, "row", 1)
    depth, flow_rows, flow_cols = steps_call("all", common + (shift_rows,))
    devices = lax.axis_size("row") * lax.axis_size("col")
    cells = inlet_cell[0, 0]
    cell_row, cell_col = cells // tile_cols, cells % tile_cols
    picked = pick_rows(cell_col // LANES * tile_rows + cell_row, depth)
    lane = jnp.arange(LANES, dtype=jnp.int32)
    chosen = jnp.sum(jnp.where(lane[None, :] == (cell_col % LANES)[:, None], picked, 0.0), axis=1)
    captured = inlet_coef[0, 0] * jnp.maximum(chosen, 0.0)
    node = inlet_node[0, 0]
    owner = (node // NODE_DEV)[None, :] == jnp.arange(devices, dtype=jnp.int32)[:, None]
    within = (node % NODE_DEV)[None, :] == jnp.arange(NODE_DEV, dtype=jnp.int32)[:, None]
    partial_value = lax.dot_general(
        jnp.where(owner, captured[None, :], 0.0), within.astype(jnp.float32), (((1,), (1,)), ((), ())),
        precision=lax.Precision.HIGHEST)
    node_inflow = lax.psum_scatter(partial_value.reshape(-1), ("row", "col"), scatter_dimension=0, tiled=True)
    return (depth, flow_rows, flow_cols, node_inflow, moved_rows, moved_cols)


def solution(mesh):
    return jax.shard_map(
        body,
        mesh=mesh,
        in_specs=(
            P("row", "col"),
            P("row", "col"),
            P("row", "col"),
            P("row", "col"),
            P("row", "col"),
            P("row", "col", None),
            P("row", "col", None),
            P("row", "col", None),
            P("row", "col"),
            P("row", "col"),
        ),
        out_specs=(
            P("row", "col"),
            P("row", "col"),
            P("row", "col"),
            P(("row", "col")),
            P(None, "row", "col"),
            P(None, "row", "col"),
        ),
        check_vma=False,
    )
```

time: 232 us -> 270 us (1.16)
  Pallas kernels: 0 us -> 166 us
  other arithmetic: 77.7 us -> 3.86 us
  local copies, waits for them, and re-layouts: 61.3 us -> 33.9 us
  starting transfers between devices: 43.9 us -> 20.2 us
  waiting for transfers between devices: 4.84 us -> 1.27 us
    pallas_call x0 -> x4, Pallas kernels: none -> 166 us  [the longest x3 160 us: steps_call(): pl.pallas_call(functools.partial(steps_kernel, cs, row0, rows, kind), out...]
    select_n x7 -> x2, other arithmetic: 42.8 us -> 0.06 us  [the longest x1 0.04 us: body(): cell_col % LANES]
    ppermute x14 -> x6, starting transfers between devices: 43.9 us -> 20.2 us  [passed_along(): lax.ppermute(value, axis, [(source, source + steps) for source in range(l...]
    gather x1 -> x0, local copies, waits for them, and re-layouts: 23 us -> none  [body(): captured = inlet_coef[0, 0] * jnp.maximum(depth.reshape(-1)[cells], 0.0)]
    scatter-add x1 -> x0, other arithmetic: 22.2 us -> none  [body(): jax.ops.segment_sum(captured, inlet_node[0, 0], num_segments=NODE_DEV * d...]
    slice x25 -> x4, local copies, waits for them, and re-layouts: 23.9 us -> 5.16 us  [columns(): x[:, start:start + EDGE]]
    unnamed x36 -> x43, local copies, waits for them, and re-layouts: 10.5 us -> 24.1 us
    add x3 -> x0, other arithmetic: 11.5 us -> none  [body(): eta = ground + depth]
  transfers between devices with their start and end apart: 14 -> 6, of which waited for: 5 -> 1; matrix products, arithmetic and copies ran while one was open for 32% -> 4% of each run, Pallas kernels for 0% -> 52%
where the time goes in v1:
time: 270 us; the launch traced here: 269 us
  Pallas kernels  166 us (61%)
  blocking collectives  40.5 us (15%)
  local copies, waits for them, and re-layouts  33.9 us (13%)
  starting transfers between devices  20.2 us (7%)
  other arithmetic  3.86 us (1%)
  between operations  2.83 us (1%)
    pallas_call x3, Pallas kernels, steps_call(): pl.pallas_call(functools.partial(steps_kernel, cs, row0, rows, kind), out...  160 us
    unnamed x1, blocking collectives  40.5 us
    unnamed x43, local copies, waits for them, and re-layouts  24.1 us
    ppermute x6, starting transfers between devices, passed_along(): lax.ppermute(value, axis, [(source, source + steps) for source in range(l...  20.2 us
    pallas_call x1, Pallas kernels, pick_rows(): pl.pallas_call(pick_kernel, out_shape=jax.ShapeDtypeStruct((count, LANES)...  5.64 us
  transfers between devices with their start and end apart: 6, of which 1 were waited for; matrix products, arithmetic and copies ran while one was open for 4% of the time, Pallas kernels for 52%

profile of v1, /device:TPU:0, one launch (start us, length us, event | category | flops | bytes accessed | tf_op | source)
XLA Modules:
  0.0 269.3 jit_solution(6743059910567408538)
XLA Ops:
  0.6 1.4 constant_dynamic-update-slice_fusion.9
  2.7 1.4 constant_dynamic-update-slice_fusion.8
  4.1 1.4 constant_dynamic-update-slice_fusion.7
  5.5 1.4 constant_dynamic-update-slice_fusion.6
  6.9 0.6 constant_dynamic-update-slice_fusion
  7.5 2.4 collective-permute-start
  9.9 0.6 constant_dynamic-update-slice_fusion.5
  10.5 1.3 collective-permute-start.1
  11.8 1.3 fusion.17
  13.1 1.3 fusion.16
  14.4 1.3 fusion.15
  15.7 1.3 fusion.14
  17.0 0.1 copy.30
  17.1 0.2 copy.31
  17.3 0.2 copy.32
  17.4 0.2 copy.33
  17.6 0.2 copy.34
  17.8 0.2 copy.35
  17.9 0.2 copy.36
  18.1 0.2 copy.37
  18.4 0.1 copy.20
  18.7 0.1 pad_maximum_fusion
  18.8 1.3 collective-permute-start.2
  20.1 0.1 copy.26
  20.3 0.1 pad_maximum_fusion.1
  20.4 4.9 %collective-permute-start.3 = (f32[5,4,784]{2,1,0:T(4,128)S(1)}, f32[5,4,784]{2,1,0:T(4,128)S(1)}, u32[]{:S(2)}, u32[]{:S(2)}) collective-permute-start(f32[5,4,784]{2,1,0:T(4,128)S(1)} %pad_maximum_fusion.1), channel_id=1, source_target_pairs={{0,1},{1,2},{2,3},{3,4},{4,5},{5,6},{6,7},{8,9},{9,10},{10,11},{11... | collective-permute-start | bytes 188168 | tf_op jit(solution)/shard_map/ppermute | solution.py:28
  26.1 0.6 copy.28
  26.7 1.3 collective-permute-done.3
  28.0 1.9 copy.29
  29.9 2.3 maximum_bitcast_fusion
  32.2 0.1 pad.4.refs_6_
  32.4 1.7 copy-done
  34.1 26.4 %steps_rows.1 = f32[3,256,1024]{2,1,0:T(8,128)} custom-call(f32[768,1024]{1,0:T(8,128)S(1)} %copy-done, f32[768,1024]{1,0:T(8,128)S(1)} %copy-done.2, f32[768,1024]{1,0:T(8,128)} %refs_2_.5, f32[768,1024]{1,0:T(8,128)} %refs_3_.5, f32[5,8,1024]{2,1,0:T(8,128)S(1)} %collective-permute-done.refs_4_, f32[5,8,1024]{2,1,0:T(8,128)S(1)} %collective-permute-done.1.refs_5_, ...), custom_call_target="tpu_custom_call" | custom-call | flops 68198400 | bytes 9547776 | tf_op jit(solution)/shard_map/steps_rows/pallas_call | solution.py:194
  60.5 4.6 %collective-permute-start.4 = (f32[3,256,1024]{2,1,0:T(8,128)}, f32[3,256,1024]{2,1,0:T(8,128)}, u32[]{:S(2)}, u32[]{:S(2)}) collective-permute-start(f32[3,256,1024]{2,1,0:T(8,128)} %steps_rows.1), channel_id=1, source_target_pairs={{0,8},{8,16},{16,24},{1,9},{9,17},{17,25},{2,10},{10,18},{18,26},{... | collective-permute-start | bytes 9437192 | tf_op jit(solution)/shard_map/ppermute | solution.py:28
  65.8 63.3 %steps_cols.1 = f32[3,768,256]{2,1,0:T(8,128)} custom-call(f32[768,1024]{1,0:T(8,128)S(1)} %copy-done, f32[768,1024]{1,0:T(8,128)S(1)} %copy-done.2, f32[768,1024]{1,0:T(8,128)S(1)} %copy-done.4, f32[768,1024]{1,0:T(8,128)} %refs_3_.5, f32[5,8,1024]{2,1,0:T(8,128)S(1)} %collective-permute-done.refs_4_, f32[5,8,1024]{2,1,0:T(8,128)S(1)} %collective-permute-done.1.refs_5_, ...), custom_call_target="tpu_custom_call" | custom-call | flops 81920000 | bytes 11468800 | tf_op jit(solution)/shard_map/steps_cols/pallas_call | solution.py:194
  129.1 5.8 %collective-permute-start.5 = (f32[3,768,256]{2,1,0:T(8,128)}, f32[3,768,256]{2,1,0:T(8,128)}, u32[]{:S(2)}, u32[]{:S(2)}) collective-permute-start(f32[3,768,256]{2,1,0:T(8,128)} %steps_cols.1), channel_id=1, source_target_pairs={{0,1},{1,2},{2,3},{3,4},{4,5},{5,6},{6,7},{8,9},{9,10},{10,11},{11... | collective-permute-start | bytes 7077896 | tf_op jit(solution)/shard_map/ppermute | solution.py:28
  135.0 1.9 copy-done.1
  136.9 1.9 copy-done.3
  138.8 1.9 copy-done.5
  140.7 70.7 %steps_all.1 = (f32[768,1024]{1,0:T(8,128)}, f32[768,1024]{1,0:T(8,128)}, f32[768,1024]{1,0:T(8,128)}) custom-call(f32[768,1024]{1,0:T(8,128)S(1)} %copy-done.1, f32[768,1024]{1,0:T(8,128)S(1)} %copy-done.3, f32[768,1024]{1,0:T(8,128)S(1)} %copy-done.5, f32[768,1024]{1,0:T(8,128)} %refs_3_.5, f32[5,8,1024]{2,1,0:T(8,128)S(1)} %collective-permute-done.refs_4_, ...), custom_call_target="tpu_custom_call" | custom-call | flops 184320000 | bytes 25804800 | tf_op jit(solution)/shard_map/steps_all/pallas_call | solution.py:194
  211.4 1.9 copy-done.6
  213.3 5.6 %pick_rows.1 = f32[4096,128]{1,0:T(8,128)S(1)} custom-call(s32[4096]{0:T(1024)S(1)} %get-tuple-element.35.spots, f32[768,1024]{1,0:T(8,128)S(1)} %copy-done.6), custom_call_target="tpu_custom_call" | custom-call | bytes 6291456 | tf_op jit(solution)/shard_map/pick_rows/pallas_call | solution.py:229
  218.9 1.3 select_reduce_fusion
  220.3 0.7 fusion
  221.0 40.5 %all-reduce.1 = f32[2048]{0:T(1024)S(1)} all-reduce(f32[2048]{0:T(1024)S(1)} %reshape.105), channel_id=2, replica_groups=mesh['row'=4,'col'=8] {'row','col'}, use_global_device_ids=true, to_apply=%region_1.2.clone | all-reduce | flops 2048 | bytes 16384
  261.5 0.6 dynamic-slice
  262.1 4.0 %copy.59 = f32[3,256,1024]{2,1,0:T(8,128)} copy(f32[3,256,1024]{2,1,0:T(8,128)} %collective-permute-done.4) | data formatting | bytes 6291456
  266.0 3.2 %copy.60 = f32[3,768,256]{2,1,0:T(8,128)} copy(f32[3,768,256]{2,1,0:T(8,128)} %collective-permute-done.5) | data formatting | bytes 4718592
  (40 shorter events, 0.7 us)
Async XLA Ops:
  7.5 10.8 %collective-permute-start = (f32[5,8,1024]{2,1,0:T(8,128)}, f32[5,8,1024]{2,1,0:T(8,128)S(1)}, u32[]{:S(2)}, u32[]{:S(2)}) collective-permute-start(f32[5,8,1024]{2,1,0:T(8,128)} %constant_dynamic-update-slice_fusion), channel_id=1, source_target_pairs={{0,8},{8,16},{16,24},{1,9},{9,17},{17,25},{2,10},{10,18},{18,26},{... | collective-permute-start | bytes 491528 | tf_op jit(solution)/shard_map/ppermute | solution.py:28
  10.5 8.0 %collective-permute-start.1 = (f32[5,8,1024]{2,1,0:T(8,128)}, f32[5,8,1024]{2,1,0:T(8,128)S(1)}, u32[]{:S(2)}, u32[]{:S(2)}) collective-permute-start(f32[5,8,1024]{2,1,0:T(8,128)} %constant_dynamic-update-slice_fusion.5), channel_id=1, source_target_pairs={{8,0},{16,8},{24,16},{9,1},{17,9},{25,17},{10,2},{18,10},{26,18},{... | collective-permute-start | bytes 491528 | tf_op jit(solution)/shard_map/ppermute | solution.py:28
  18.8 7.2 %collective-permute-start.2 = (f32[5,4,784]{2,1,0:T(4,128)S(1)}, f32[5,4,784]{2,1,0:T(4,128)S(1)}, u32[]{:S(2)}, u32[]{:S(2)}) collective-permute-start(f32[5,4,784]{2,1,0:T(4,128)S(1)} %pad_maximum_fusion), channel_id=1, source_target_pairs={{1,0},{2,1},{3,2},{4,3},{5,4},{6,5},{7,6},{9,8},{10,9},{11,10},{12... | collective-permute-start | bytes 188168 | tf_op jit(solution)/shard_map/ppermute | solution.py:28
  20.4 7.5 %collective-permute-start.3 = (f32[5,4,784]{2,1,0:T(4,128)S(1)}, f32[5,4,784]{2,1,0:T(4,128)S(1)}, u32[]{:S(2)}, u32[]{:S(2)}) collective-permute-start(f32[5,4,784]{2,1,0:T(4,128)S(1)} %pad_maximum_fusion.1), channel_id=1, source_target_pairs={{0,1},{1,2},{2,3},{3,4},{4,5},{5,6},{6,7},{8,9},{9,10},{10,11},{11... | collective-permute-start | bytes 188168 | tf_op jit(solution)/shard_map/ppermute | solution.py:28
  29.9 2.5 copy-start.2
  32.2 1.9 copy-start
  34.1 31.7 %copy-start.4 = (f32[768,1024]{1,0:T(8,128)S(1)}, f32[768,1024]{1,0:T(8,128)}, u32[]{:S(2)}) copy-start(f32[768,1024]{1,0:T(8,128)} %refs_2_.5) | copy-start | bytes 9437188
  60.5 201.6 %collective-permute-start.4 = (f32[3,256,1024]{2,1,0:T(8,128)}, f32[3,256,1024]{2,1,0:T(8,128)}, u32[]{:S(2)}, u32[]{:S(2)}) collective-permute-start(f32[3,256,1024]{2,1,0:T(8,128)} %steps_rows.1), channel_id=1, source_target_pairs={{0,8},{8,16},{16,24},{1,9},{9,17},{17,25},{2,10},{10,18},{18,26},{... | collective-permute-start | bytes 9437192 | tf_op jit(solution)/shard_map/ppermute | solution.py:28
  65.8 69.1 %copy-start.7 = (s32[1,1,4096]{2,1,0:T(1,128)S(1)}, s32[1,1,4096]{2,1,0:T(1,128)}, u32[]{:S(2)}) copy-start(s32[1,1,4096]{2,1,0:T(1,128)} %param.15) | copy-start | bytes 49156
  65.8 69.1 %copy-start.8 = (s32[1,1,4096]{2,1,0:T(1,128)S(1)}, s32[1,1,4096]{2,1,0:T(1,128)}, u32[]{:S(2)}) copy-start(s32[1,1,4096]{2,1,0:T(1,128)} %param.16) | copy-start | bytes 49156
  129.1 132.9 %collective-permute-start.5 = (f32[3,768,256]{2,1,0:T(8,128)}, f32[3,768,256]{2,1,0:T(8,128)}, u32[]{:S(2)}, u32[]{:S(2)}) collective-permute-start(f32[3,768,256]{2,1,0:T(8,128)} %steps_cols.1), channel_id=1, source_target_pairs={{0,1},{1,2},{2,3},{3,4},{4,5},{5,6},{6,7},{8,9},{9,10},{10,11},{11... | collective-permute-start | bytes 7077896 | tf_op jit(solution)/shard_map/ppermute | solution.py:28
  135.0 1.9 copy-start.1
  136.9 1.9 copy-start.3
  138.8 1.9 copy-start.5
  211.4 1.9 copy-start.6
  213.3 6.9 %copy-start.9 = (f32[1,1,4096]{2,1,0:T(1,128)S(1)}, f32[1,1,4096]{2,1,0:T(1,128)}, u32[]{:S(2)}) copy-start(f32[1,1,4096]{2,1,0:T(1,128)} %param.17) | copy-start | bytes 49156

commit v2 on v1

v2 whole, which is shorter than its diff:
```python
import functools
import math

import jax
import jax.numpy as jnp
from jax import lax
from jax.experimental import pallas as pl
from jax.experimental.pallas import tpu as pltpu
from jax.sharding import PartitionSpec as P

STEPS = 3
BLOCK = 128
MAX_BLOCKS = 2
NODE_DEV = 64
LANES = 128
SUB = 8
EDGE = 4


gravity = 9.81
time_step = 0.1
friction = 0.0025
depth_floor = 0.25
POWER = -7.0 / (3.0 * math.log(2.0))


def passed_along(value, axis, steps):
    count = lax.axis_size(axis)
    leading, last = (max(0, -steps), min(count, count - steps))
    return lax.ppermute(value, axis, [(source, source + steps) for source in range(leading, last)])


def face_update(flow, eta, eta_next, top_ground):
    face_depth = jnp.maximum(jnp.maximum(eta, eta_next) - top_ground, 0.0)
    floored = jnp.maximum(face_depth, depth_floor)
    root = jnp.exp2(POWER * jnp.log(floored))
    drag = (gravity * time_step * friction) * jnp.abs(flow) * root
    pushed = flow - (gravity * time_step) * face_depth * (eta_next - eta)
    return pushed / (1.0 + drag)


def steps_kernel(cs, row0, rows, kind, group, *refs):
    depth, ground, frow, fcol, top, bottom, side, wet, shift = refs[:9]
    if kind == "all":
        outs, scratch = refs[9:12], refs[12:]
    else:
        if kind == "rows":
            refs = refs[:9] + refs[10:]
        outs, scratch = refs[9:10], refs[10:]
    d, g, f, c, w8, zc, zero, in_sem, out_sem = scratch
    n = len(cs)
    high = rows - row0 + 32
    arrays = ((depth, d), (ground, g), (frow, f), (fcol, c))
    copies = []
    for a, (src, dst) in enumerate(arrays):
        for i, slab in enumerate(cs[:-1]):
            copies.append(pltpu.make_async_copy(
                src.at[pl.ds(row0, rows - row0), pl.ds(slab * LANES, LANES)],
                dst.at[pl.ds(i * high + 16, rows - row0)], in_sem.at[a, i]))
    for copy in copies:
        copy.start()
    blank = jnp.zeros((SUB, LANES), jnp.float32)
    for a, (_, dst) in enumerate(arrays):
        for i in range(n - 1):
            lanes = pl.ds(cs[i] * LANES, LANES)
            dst[pl.ds(i * high, SUB), :] = blank
            dst[pl.ds(i * high + 8, SUB), :] = top[pl.ds(a * SUB, SUB), lanes] if row0 == 0 else blank
            dst[pl.ds(i * high + high - 16, SUB), :] = bottom[pl.ds(a * SUB, SUB), lanes]
            dst[pl.ds(i * high + high - 8, SUB), :] = blank
    mixed = side[pl.ds(row0 + LANES - 16, high), :]
    for a, dst in enumerate((d, g, f, c, w8)):
        base = (n - 1) * high if a < 4 else 0
        dst[pl.ds(base, high), :] = pltpu.roll(mixed, LANES - 8 * a - EDGE, 1)
    if kind != "all":
        zero[...] = jnp.zeros_like(zero)
    for copy in copies:
        copy.wait()

    lane = lax.broadcasted_iota(jnp.int32, (SUB, LANES), 1)
    at_last, at_first = lane == LANES - 1, lane == 0
    at_top = lax.broadcasted_iota(jnp.int32, (SUB, LANES), 0) == 0

    def rightward(vals):
        rolled = [pltpu.roll(v, LANES - 1, 1) for v in vals]
        return [jnp.where(at_last, rolled[(i + 1) % n], rolled[i]) for i in range(n)]

    def leftward(vals):
        rolled = [pltpu.roll(v, 1, 1) for v in vals]
        return [jnp.where(at_first, rolled[(i - 1) % n], rolled[i]) for i in range(n)]

    first = 1 if row0 == 0 else 2
    last = high // SUB - 2
    sizes = [i * high for i in range(n)]

    def bed(b, carry):
        r = pl.multiple_of(b * SUB, SUB)
        vals = [g[pl.ds(s + r, SUB), :] for s in sizes]
        for s, v, q in zip(sizes, vals, rightward(vals)):
            zc[pl.ds(s + r, SUB), :] = jnp.maximum(v, q)
        return carry

    lax.fori_loop(first, last + 1, bed, 0)
    active = jnp.broadcast_to(wet[0, 0], (SUB, LANES)) > 0
    top_active = top[pl.ds(4 * SUB, SUB), pl.ds(0, LANES)] > 0.0
    bottom_active = bottom[pl.ds(4 * SUB, SUB), pl.ds(0, LANES)] > 0.0

    def block(b, count, mask, carry):
        r = b * SUB if isinstance(b, int) else pl.multiple_of(b * SUB, SUB)
        pairs = [(i, j) for j in range(count) for i in range(n)]
        at = {(i, j): sizes[i] + r + j * SUB for i, j in pairs}
        load = lambda ref, off=0: {p: ref[pl.ds(at[p] + off, SUB), :] for p in pairs}
        depths, grounds, depths_below, grounds_below = load(d), load(g), load(d, 1), load(g, 1)
        beds, old_f, old_c = load(zc), load(f), load(c)
        halo = [w8[pl.ds(r + j * SUB, SUB), :] > 0.0 for j in range(count)]
        carry = list(carry)
        done = {}
        for j in range(count):
            masks = [mask] * (n - 1) + [halo[j]]
            eta = [depths[i, j] + grounds[i, j] for i in range(n)]
            right = rightward(eta)
            cols = []
            for i in range(n):
                new = face_update(old_c[i, j], eta[i], right[i], beds[i, j])
                cols.append(jnp.where(masks[i], new, old_c[i, j]))
            before = leftward(cols)
            for i in range(n):
                below = grounds_below[i, j]
                new = face_update(old_f[i, j], eta[i], depths_below[i, j] + below, jnp.maximum(grounds[i, j], below))
                new = jnp.where(masks[i], new, old_f[i, j])
                turned = pltpu.roll(new, 1, 0)
                above = jnp.where(at_top, carry[i], turned)
                carry[i] = turned
                moved = depths[i, j] + time_step * (above - new + before[i] - cols[i])
                done[i, j] = (jnp.where(masks[i], moved, depths[i, j]), new, cols[i])
        for p in pairs:
            for ref, value in zip((d, f, c), done[p]):
                ref[pl.ds(at[p], SUB), :] = value
        return tuple(carry)

    for _ in range(STEPS):
        carry = (blank,) * n
        if row0 == 0:
            carry = block(1, 1, top_active, carry)
        carry = lax.fori_loop(0, (last - 2) // group, lambda k, old: block(k * group + 2, group, active, old), carry)
        block(last, 1, bottom_active, carry)

    span = MAX_BLOCKS * BLOCK
    state = (d, f, c)
    copies = []
    for a, src in enumerate(state):
        if kind == "all":
            for i, slab in enumerate(cs[:-1]):
                copies.append(pltpu.make_async_copy(
                    src.at[pl.ds(i * high + 16, rows)], outs[a].at[:, pl.ds(slab * LANES, LANES)], out_sem.at[a, i]))
                copies[-1].start()
            continue
        for k in range(MAX_BLOCKS):
            keep = k >= MAX_BLOCKS - shift[0, 0]
            if kind == "cols":
                pieces = [(src.at[pl.ds((n - 1 - MAX_BLOCKS + k) * high + 16, rows)], zero,
                           outs[0].at[a, :, pl.ds(k * BLOCK, BLOCK)], k)]
            else:
                pieces = [(src.at[pl.ds(i * high + high - 16 - span + k * BLOCK, BLOCK)], zero,
                           outs[0].at[a, pl.ds(k * BLOCK, BLOCK), pl.ds(slab * LANES, LANES)], k * n + i)
                          for i, slab in enumerate(cs[:-1])]
            for data, empty, dst, m in pieces:
                copy = pltpu.make_async_copy(data, dst, out_sem.at[a, m])
                hole = pltpu.make_async_copy(empty, dst, out_sem.at[a, m])
                pl.when(keep)(copy.start)
                pl.when(jnp.logical_not(keep))(hole.start)
                copies.append(copy)
    for copy in copies:
        copy.wait()


def steps_call(kind, args):
    rows, width = args[0].shape
    slabs = width // LANES
    cs, row0, group = list(range(slabs + 1)), 0, 2
    span = MAX_BLOCKS * BLOCK
    if kind == "cols":
        cs, group = cs[slabs - MAX_BLOCKS - 1:], 4
        out = [jax.ShapeDtypeStruct((3, rows, span), jnp.float32)]
        zero, sems = (rows, LANES), MAX_BLOCKS
    elif kind == "rows":
        row0 = rows - span - 2 * SUB
        out = [jax.ShapeDtypeStruct((3, span, width), jnp.float32)]
        zero, sems = (BLOCK, LANES), MAX_BLOCKS * len(cs)
    else:
        out = [jax.ShapeDtypeStruct((rows, width), jnp.float32)] * 3
        zero, sems = (SUB, LANES), len(cs)
    n, high = len(cs), rows - row0 + 32
    anywhere = pl.BlockSpec(memory_space=pltpu.HBM)
    vmem = pl.BlockSpec(memory_space=pltpu.VMEM)
    smem = pl.BlockSpec(memory_space=pltpu.SMEM)
    buffer = pltpu.VMEM((n * high, LANES), jnp.float32)
    cells = n * high * LANES
    return pl.pallas_call(
        functools.partial(steps_kernel, cs, row0, rows, kind, group),
        out_shape=out,
        in_specs=[anywhere] * 4 + [vmem, vmem, vmem, smem, smem] + [anywhere] * (kind == "rows"),
        out_specs=[anywhere] * len(out),
        scratch_shapes=[buffer] * 4 + [pltpu.VMEM((high, LANES), jnp.float32), buffer, pltpu.VMEM(zero, jnp.float32),
                                       pltpu.SemaphoreType.DMA((4, n)), pltpu.SemaphoreType.DMA((3, sems))],
        compiler_params=pltpu.CompilerParams(vmem_limit_bytes=58 << 20),
        cost_estimate=pl.CostEstimate(flops=cells, transcendentals=0, bytes_accessed=cells),
        name="steps_" + kind,
    )(*args)


def pick_kernel(spots, depth, out, slabs, sem):
    rows, width = depth.shape
    copies = [pltpu.make_async_copy(depth.at[:, pl.ds(i * LANES, LANES)], slabs.at[pl.ds(i * rows, rows)], sem.at[i])
              for i in range(width // LANES)]
    for copy in copies:
        copy.start()
    for copy in copies:
        copy.wait()

    def body(k, carry):
        base = pl.multiple_of(k * 16, 16)
        for j in range(16):
            out[pl.ds(base + j, 1), :] = slabs[pl.ds(spots[base + j], 1), :]
        return carry

    lax.fori_loop(0, out.shape[0] // 16, body, 0)


def pick_rows(spots, depth):
    rows, width = depth.shape
    count = spots.shape[0]
    return pl.pallas_call(
        pick_kernel,
        out_shape=jax.ShapeDtypeStruct((count, LANES), jnp.float32),
        in_specs=[pl.BlockSpec(memory_space=pltpu.SMEM), pl.BlockSpec(memory_space=pltpu.HBM)],
        out_specs=pl.BlockSpec(memory_space=pltpu.VMEM),
        scratch_shapes=[pltpu.VMEM((rows * width // LANES, LANES), jnp.float32),
                        pltpu.SemaphoreType.DMA((width // LANES,))],
        compiler_params=pltpu.CompilerParams(vmem_limit_bytes=58 << 20),
        cost_estimate=pl.CostEstimate(flops=0, transcendentals=0, bytes_accessed=8 * rows * width),
        name="pick_rows",
    )(spots, depth)


def halo_kernel(counts, depth, ground, frow, fcol, wet, top, bottom, side,
                low, high, packed, near, far, got_top, got_bottom, got_left, got_right,
                load_sem, send_sem, recv_sem):
    rows, width = depth.shape
    me_row, me_col = lax.axis_index("row"), lax.axis_index("col")
    moves = [(-1, 0), (1, 0), (0, -1), (0, 1), (-1, -1), (-1, 1), (1, -1), (1, 1)]

    def there(dr, dc):
        r, q = me_row + dr, me_col + dc
        inside = jnp.logical_and(jnp.logical_and(r >= 0, r < counts[0]), jnp.logical_and(q >= 0, q < counts[1]))
        return inside, (r, q)

    for ref in (got_top, got_bottom, got_left, got_right):
        ref[...] = jnp.zeros_like(ref)
    barrier = pltpu.get_barrier_semaphore()
    for move in moves:
        inside, device = there(*move)

        @pl.when(inside)
        def _():
            pl.semaphore_signal(barrier, inc=1, device_id=device, device_id_type=pl.DeviceIdType.MESH)

    copies = []
    for a, src in enumerate((depth, ground, frow, fcol)):
        for k, (piece, dst) in enumerate((
            (src.at[pl.ds(0, SUB), :], near.at[pl.ds(a * SUB, SUB), :]),
            (src.at[pl.ds(rows - SUB, SUB), :], far.at[pl.ds(a * SUB, SUB), :]),
            (src.at[:, pl.ds(0, LANES)], low.at[a]),
            (src.at[:, pl.ds(width - LANES, LANES)], high.at[a]),
        )):
            copies.append(pltpu.make_async_copy(piece, dst, load_sem.at[a, k]))
            copies[-1].start()
    flag = jnp.broadcast_to(wet[0, 0], (SUB, width)).astype(jnp.float32)
    near[pl.ds(4 * SUB, SUB), :] = flag
    far[pl.ds(4 * SUB, SUB), :] = flag
    for copy in copies:
        copy.wait()
    lane = lax.broadcasted_iota(jnp.int32, (LANES, LANES), 1)
    for k in range(rows // LANES):
        part = pl.ds(k * LANES, LANES)
        merged = jnp.broadcast_to(wet[0, 0], (LANES, LANES)).astype(jnp.float32)
        for a in reversed(range(4)):
            ends = jnp.where(lane < LANES // 2, low[a, part, :], high[a, part, :])
            merged = jnp.where(lane < 8 * a + 8, pltpu.roll(ends, 8 * a + EDGE, 1), merged)
        packed[:, part] = merged.T[:5 * SUB, :]

    pl.semaphore_wait(barrier, sum(there(*move)[0].astype(jnp.int32) for move in moves))

    mid = pl.ds(LANES, rows)
    start, end = pl.ds(0, LANES), pl.ds(rows - LANES, LANES)
    above, under = pl.ds(0, LANES), pl.ds(rows + LANES, LANES)
    plan = [
        (near, got_bottom), (far, got_top), (packed, got_right.at[:, mid]), (packed, got_left.at[:, mid]),
        (packed.at[:, start], got_right.at[:, under]), (packed.at[:, start], got_left.at[:, under]),
        (packed.at[:, end], got_right.at[:, above]), (packed.at[:, end], got_left.at[:, above]),
    ]
    sends = []
    for k, (move, (src, dst)) in enumerate(zip(moves, plan)):
        inside, device = there(*move)
        copy = pltpu.make_async_remote_copy(src, dst, send_sem.at[k], recv_sem.at[k], device_id=device,
                                            device_id_type=pl.DeviceIdType.MESH)
        pl.when(inside)(copy.start)
        sends.append((inside, there(-move[0], -move[1])[0], copy))
    for sent, fed, copy in sends:
        pl.when(sent)(copy.wait_send)
        pl.when(fed)(copy.wait_recv)
    top[...] = got_top[...]
    bottom[...] = got_bottom[...]
    from_right = lax.broadcasted_iota(jnp.int32, (5 * SUB, LANES), 0) % SUB >= EDGE
    rest = jnp.zeros((LANES - 5 * SUB, LANES), jnp.float32)
    for k in range(rows // LANES + 2):
        part = pl.ds(k * LANES, LANES)
        both = jnp.where(from_right, got_right[:, part], got_left[:, part])
        side[part, :] = jnp.concatenate([both, rest], axis=0).T


def halos(arrays, wet):
    rows, width = arrays[0].shape
    counts = (lax.axis_size("row"), lax.axis_size("col"))
    across, along = (5 * SUB, width), (5 * SUB, rows + 2 * LANES)
    vmem = lambda shape: pltpu.VMEM(shape, jnp.float32)
    return pl.pallas_call(
        functools.partial(halo_kernel, counts),
        out_shape=[jax.ShapeDtypeStruct(across, jnp.float32)] * 2 + [
            jax.ShapeDtypeStruct((rows + 2 * LANES, LANES), jnp.float32)],
        in_specs=[pl.BlockSpec(memory_space=pltpu.HBM)] * 4 + [pl.BlockSpec(memory_space=pltpu.SMEM)],
        out_specs=[pl.BlockSpec(memory_space=pltpu.VMEM)] * 3,
        scratch_shapes=[vmem((4, rows, LANES)), vmem((4, rows, LANES)), vmem((5 * SUB, rows)), vmem(across), vmem(across),
                        vmem(across), vmem(across), vmem(along), vmem(along),
                        pltpu.SemaphoreType.DMA((4, 4)), pltpu.SemaphoreType.DMA((8,)), pltpu.SemaphoreType.DMA((8,))],
        compiler_params=pltpu.CompilerParams(collective_id=0, has_side_effects=True, vmem_limit_bytes=58 << 20),
        name="halos",
    )(*arrays, wet)


def owners_kernel(counts, parts, total, slots, send_sem, recv_sem):
    n_row, n_col = counts
    devices = n_row * n_col
    me = lax.axis_index("row") * n_col + lax.axis_index("col")
    barrier = pltpu.get_barrier_semaphore()

    def place(k):
        other = lax.rem(me + k, devices)
        return other, (other // n_col, lax.rem(other, n_col))

    @pl.loop(1, devices)
    def _(k):
        pl.semaphore_signal(barrier, inc=1, device_id=place(k)[1], device_id_type=pl.DeviceIdType.MESH)

    pl.semaphore_wait(barrier, devices - 1)

    def send(k):
        other, device = place(k)
        return pltpu.make_async_remote_copy(parts.at[other], slots.at[k], send_sem.at[k], recv_sem.at[k],
                                            device_id=device, device_id_type=pl.DeviceIdType.MESH)

    @pl.loop(1, devices)
    def _(k):
        send(k).start()

    @pl.loop(1, devices)
    def _(k):
        send(k).wait()

    total[...] = parts[me] + jnp.sum(slots[pl.ds(1, devices - 1)], axis=0)


def to_owners(parts):
    counts = (lax.axis_size("row"), lax.axis_size("col"))
    devices = counts[0] * counts[1]
    return pl.pallas_call(
        functools.partial(owners_kernel, counts),
        out_shape=jax.ShapeDtypeStruct((1, LANES), jnp.float32),
        in_specs=[pl.BlockSpec(memory_space=pltpu.VMEM)],
        out_specs=pl.BlockSpec(memory_space=pltpu.VMEM),
        scratch_shapes=[pltpu.VMEM((devices, 1, LANES), jnp.float32), pltpu.SemaphoreType.DMA((devices,)),
                        pltpu.SemaphoreType.DMA((devices,))],
        compiler_params=pltpu.CompilerParams(collective_id=1, has_side_effects=True, vmem_limit_bytes=58 << 20),
        name="to_owners",
    )(parts)


def body(
    depth,
    ground,
    flow_rows,
    flow_cols,
    wet_tiles,
    inlet_cell,
    inlet_node,
    inlet_coef,
    shift_rows,
    shift_cols,
):
    tile_rows, tile_cols = depth.shape
    arrays = (depth, ground, flow_rows, flow_cols)
    top, bottom, side = halos(arrays, wet_tiles)
    common = arrays + (top, bottom, side, wet_tiles)
    (edge_cols,) = steps_call("cols", common + (shift_cols,))
    moved_cols = passed_along(edge_cols, "col", 1)
    (edge_rows,) = steps_call("rows", common + (shift_rows, edge_cols))
    moved_rows = passed_along(edge_rows, "row", 1)
    depth, flow_rows, flow_cols = steps_call("all", common + (shift_rows,))
    devices = lax.axis_size("row") * lax.axis_size("col")
    cells = inlet_cell[0, 0]
    cell_row, cell_col = cells // tile_cols, cells % tile_cols
    picked = pick_rows(cell_col // LANES * tile_rows + cell_row, depth)
    lane = jnp.arange(LANES, dtype=jnp.int32)
    chosen = jnp.sum(jnp.where(lane[None, :] == (cell_col % LANES)[:, None], picked, 0.0), axis=1)
    captured = inlet_coef[0, 0] * jnp.maximum(chosen, 0.0)
    node = inlet_node[0, 0]
    owner = (node // NODE_DEV)[None, :] == jnp.arange(devices, dtype=jnp.int32)[:, None]
    within = (node % NODE_DEV)[None, :] == jnp.arange(LANES, dtype=jnp.int32)[:, None]
    partial_value = lax.dot_general(
        jnp.where(owner, captured[None, :], 0.0), within.astype(jnp.float32), (((1,), (1,)), ((), ())),
        precision=lax.Precision.HIGHEST)
    node_inflow = to_owners(partial_value[:, None, :])[0, :NODE_DEV]
    return (depth, flow_rows, flow_cols, node_inflow, moved_rows, moved_cols)


def solution(mesh):
    return jax.shard_map(
        body,
        mesh=mesh,
        in_specs=(
            P("row", "col"),
            P("row", "col"),
            P("row", "col"),
            P("row", "col"),
            P("row", "col"),
            P("row", "col", None),
            P("row", "col", None),
            P("row", "col", None),
            P("row", "col"),
            P("row", "col"),
        ),
        out_specs=(
            P("row", "col"),
            P("row", "col"),
            P("row", "col"),
            P(("row", "col")),
            P(None, "row", "col"),
            P(None, "row", "col"),
        ),
        check_vma=False,
    )
```

time: 270 us -> 149 us (0.55)
  blocking collectives: 40.5 us -> 0 us
  Pallas kernels: 166 us -> 126 us
  local copies, waits for them, and re-layouts: 33.9 us -> 6.07 us
  starting transfers between devices: 20.2 us -> 7.95 us
    pallas_call x3 -> x5, Pallas kernels: 160 us -> 118 us  [the longest x3 95.6 us: steps_call(): pl.pallas_call(functools.partial(steps_kernel, cs, row0, rows, kind, grou...]
    unnamed x1 -> x0, blocking collectives: 40.5 us -> none
    unnamed x43 -> x10, local copies, waits for them, and re-layouts: 24.1 us -> 4.91 us
    ppermute x6 -> x2, starting transfers between devices: 20.2 us -> 7.95 us  [passed_along(): lax.ppermute(value, axis, [(source, source + steps) for source in range(l...]
    slice x4 -> x0, local copies, waits for them, and re-layouts: 5.16 us -> none  [columns(): x[:, start:start + EDGE]]
    pallas_call x1, Pallas kernels: 5.64 us -> 8.75 us  [pick_rows(): pl.pallas_call(pick_kernel, out_shape=jax.ShapeDtypeStruct((count, LANES)...]
  transfers between devices with their start and end apart: 6 -> 2, of which waited for: 1 -> 0; matrix products, arithmetic and copies ran while one was open for 4% -> 4% of each run, Pallas kernels for 52% -> 46%
where the time goes in v2:
time: 149 us; the launch traced here: 148 us
  Pallas kernels  126 us (85%)
  starting transfers between devices  7.95 us (5%)
  local copies, waits for them, and re-layouts  6.07 us (4%)
  other arithmetic  3.16 us (2%)
  between operations  2.7 us (2%)
  matrix products  1.86 us (1%)
    pallas_call x3, Pallas kernels, steps_call(): pl.pallas_call(functools.partial(steps_kernel, cs, row0, rows, kind, grou...  95.6 us
    pallas_call x1, Pallas kernels, halos(): pl.pallas_call(functools.partial(halo_kernel, counts), out_shape=[jax.Sha...  11.6 us
    pallas_call x1, Pallas kernels, to_owners(): pl.pallas_call(functools.partial(owners_kernel, counts), out_shape=jax.Sh...  10.5 us
    pallas_call x1, Pallas kernels, pick_rows(): pl.pallas_call(pick_kernel, out_shape=jax.ShapeDtypeStruct((count, LANES)...  8.75 us
    ppermute x2, starting transfers between devices, passed_along(): lax.ppermute(value, axis, [(source, source + steps) for source in range(l...  7.95 us
    unnamed x10, local copies, waits for them, and re-layouts  4.91 us
  transfers between devices with their start and end apart: 2, of which 0 were waited for; matrix products, arithmetic and copies ran while one was open for 4% of the time, Pallas kernels for 46%

profile of v2, /device:TPU:0, one launch (start us, length us, event | category | flops | bytes accessed | tf_op | source)
XLA Modules:
  0.0 148.2 jit_solution(3021334993021042928)
XLA Ops:
  2.6 11.6 %halos.1 = (f32[40,1024]{1,0:T(8,128)}, f32[40,1024]{1,0:T(8,128)}, f32[1024,128]{1,0:T(8,128)}) custom-call(f32[768,1024]{1,0:T(8,128)} %refs_0_.5, f32[768,1024]{1,0:T(8,128)} %refs_1_.5, f32[768,1024]{1,0:T(8,128)} %refs_2_.5, f32[768,1024]{1,0:T(8,128)} %refs_3_.5, s32[1,1]{1,0:T(1,128)S(6)} %copy.18.wet.refs_7_), custom_call_target="tpu_custom_call" | custom-call | tf_op jit(solution)/shard_map/halos/pallas_call | solution.py:326
  14.2 27.2 %steps_cols.1.refs_9_ = f32[3,768,256]{2,1,0:T(8,128)} custom-call(f32[768,1024]{1,0:T(8,128)} %refs_0_.5, f32[768,1024]{1,0:T(8,128)} %refs_1_.5, f32[768,1024]{1,0:T(8,128)} %refs_2_.5, f32[768,1024]{1,0:T(8,128)} %refs_3_.5, f32[40,1024]{1,0:T(8,128)} %get-tuple-element.12.refs_4_, f32[40,1024]{1,0:T(8,128)} %get-tuple-element.13.refs_5_, ...), custom_call_target="tpu_custom_call" | custom-call | flops 409600 | bytes 409600 | tf_op jit(solution)/shard_map/steps_cols/pallas_call | solution.py:198
  41.4 0.0 copy-start
  41.4 20.0 %steps_rows.1 = f32[3,256,1024]{2,1,0:T(8,128)} custom-call(f32[768,1024]{1,0:T(8,128)} %refs_0_.5, f32[768,1024]{1,0:T(8,128)} %refs_1_.5, f32[768,1024]{1,0:T(8,128)} %refs_2_.5, f32[768,1024]{1,0:T(8,128)} %refs_3_.5, f32[40,1024]{1,0:T(8,128)} %get-tuple-element.12.refs_4_, f32[40,1024]{1,0:T(8,128)} %get-tuple-element.13.refs_5_, ...), custom_call_target="tpu_custom_call" | custom-call | flops 350208 | bytes 350208 | tf_op jit(solution)/shard_map/steps_rows/pallas_call | solution.py:198
  61.4 0.0 copy-start.1
  61.4 2.7 %collective-permute-start = (f32[3,256,1024]{2,1,0:T(8,128)}, f32[3,256,1024]{2,1,0:T(8,128)S(1)}, u32[]{:S(2)}, u32[]{:S(2)}) collective-permute-start(f32[3,256,1024]{2,1,0:T(8,128)} %steps_rows.1), channel_id=1, source_target_pairs={{0,8},{8,16},{16,24},{1,9},{9,17},{17,25},{2,10},{10,18},{18,26},{... | collective-permute-start | bytes 9437192 | tf_op jit(solution)/shard_map/ppermute | solution.py:30
  64.1 0.0 copy-done
  64.1 5.3 %collective-permute-start.1 = (f32[3,768,256]{2,1,0:T(8,128)S(1)}, f32[3,768,256]{2,1,0:T(8,128)}, u32[]{:S(2)}, u32[]{:S(2)}) collective-permute-start(f32[3,768,256]{2,1,0:T(8,128)S(1)} %copy-done), channel_id=1, source_target_pairs={{0,1},{1,2},{2,3},{3,4},{4,5},{5,6},{6,7},{8,9},{9,10},{10,11},{11... | collective-permute-start | bytes 7077896 | tf_op jit(solution)/shard_map/ppermute | solution.py:30
  69.4 48.4 %steps_all.1 = (f32[768,1024]{1,0:T(8,128)}, f32[768,1024]{1,0:T(8,128)}, f32[768,1024]{1,0:T(8,128)}) custom-call(f32[768,1024]{1,0:T(8,128)} %refs_0_.5, f32[768,1024]{1,0:T(8,128)} %refs_1_.5, f32[768,1024]{1,0:T(8,128)} %refs_2_.5, f32[768,1024]{1,0:T(8,128)} %refs_3_.5, f32[40,1024]{1,0:T(8,128)} %get-tuple-element.12.refs_4_, ...), custom_call_target="tpu_custom_call" | custom-call | flops 921600 | bytes 921600 | tf_op jit(solution)/shard_map/steps_all/pallas_call | solution.py:198
  117.8 0.0 copy-done.1
  117.8 0.6 add_select_fusion.3
  118.5 0.0 copy-start.2
  118.5 0.0 copy-start.3
  118.5 8.7 %pick_rows.1 = f32[4096,128]{1,0:T(8,128)} custom-call(s32[4096]{0:T(1024)} %get-tuple-element.21.spots, f32[768,1024]{1,0:T(8,128)} %get-tuple-element.28.depth), custom_call_target="tpu_custom_call" | custom-call | bytes 6291456 | tf_op jit(solution)/shard_map/pick_rows/pallas_call | solution.py:232
  127.2 2.5 %select_reduce_fusion = f32[4096]{0:T(1024)S(1)} fusion(f32[4096,128]{1,0:T(8,128)} %pick_rows.1, s32[4096]{0:T(1024)S(1)} %get-tuple-element.20), kind=kLoop, calls=%fused_computation.1 | loop fusion | flops 1568768 | bytes 2129920 | tf_op jit(solution)/shard_map/reduce_sum | solution.py:413
  129.7 0.0 copy-done.2
  129.8 0.0 copy-done.3
  129.8 1.9 %fusion = f32[32,128]{1,0:T(8,128)} fusion(s32[4096]{0:T(1024)S(1)} %get-tuple-element.19, f32[4096]{0:T(1024)S(1)} %maximum_multiply_fusion, s32[4096]{0:T(1024)S(1)} %get-tuple-element.18), kind=kOutput, calls=%fused_computation.3 | convolution fusion | flops 202113024 | bytes 65536 | tf_op jit(solution)/shard_map/dot_general | solution.py:418
  131.7 10.5 %to_owners.1 = f32[1,128]{1,0:T(1,128)} custom-call(f32[32,1,128]{2,1,0:T(1,128)} %bitcast.9), custom_call_target="tpu_custom_call" | custom-call | tf_op jit(solution)/shard_map/to_owners/pallas_call | solution.py:375
  142.1 1.2 slice_bitcast_fusion
  143.3 0.0 collective-permute-done.1
  143.3 0.0 collective-permute-done
  143.3 1.7 %copy.21 = f32[3,256,1024]{2,1,0:T(8,128)} copy(f32[3,256,1024]{2,1,0:T(8,128)S(1)} %collective-permute-done) | data formatting | bytes 6291456
  145.0 3.2 %copy.22 = f32[3,768,256]{2,1,0:T(8,128)} copy(f32[3,768,256]{2,1,0:T(8,128)} %collective-permute-done.1) | data formatting | bytes 4718592
  (2 shorter events, 0.0 us)
Async XLA Ops:
  41.4 22.7 %copy-start = (f32[3,768,256]{2,1,0:T(8,128)S(1)}, f32[3,768,256]{2,1,0:T(8,128)}, u32[]{:S(2)}) copy-start(f32[3,768,256]{2,1,0:T(8,128)} %steps_cols.1.refs_9_) | copy-start | bytes 7077892
  61.4 56.4 %copy-start.1 = (s32[1,1,4096]{2,1,0:T(1,128)S(1)}, s32[1,1,4096]{2,1,0:T(1,128)}, u32[]{:S(2)}) copy-start(s32[1,1,4096]{2,1,0:T(1,128)} %param.15) | copy-start | bytes 49156
  61.4 81.9 %collective-permute-start = (f32[3,256,1024]{2,1,0:T(8,128)}, f32[3,256,1024]{2,1,0:T(8,128)S(1)}, u32[]{:S(2)}, u32[]{:S(2)}) collective-permute-start(f32[3,256,1024]{2,1,0:T(8,128)} %steps_rows.1), channel_id=1, source_target_pairs={{0,8},{8,16},{16,24},{1,9},{9,17},{17,25},{2,10},{10,18},{18,26},{... | collective-permute-start | bytes 9437192 | tf_op jit(solution)/shard_map/ppermute | solution.py:30
  64.1 79.2 %collective-permute-start.1 = (f32[3,768,256]{2,1,0:T(8,128)S(1)}, f32[3,768,256]{2,1,0:T(8,128)}, u32[]{:S(2)}, u32[]{:S(2)}) collective-permute-start(f32[3,768,256]{2,1,0:T(8,128)S(1)} %copy-done), channel_id=1, source_target_pairs={{0,1},{1,2},{2,3},{3,4},{4,5},{5,6},{6,7},{8,9},{9,10},{10,11},{11... | collective-permute-start | bytes 7077896 | tf_op jit(solution)/shard_map/ppermute | solution.py:30
  118.5 11.3 %copy-start.2 = (s32[1,1,4096]{2,1,0:T(1,128)S(1)}, s32[1,1,4096]{2,1,0:T(1,128)}, u32[]{:S(2)}) copy-start(s32[1,1,4096]{2,1,0:T(1,128)} %param.16) | copy-start | bytes 49156
  118.5 11.3 %copy-start.3 = (f32[1,1,4096]{2,1,0:T(1,128)S(1)}, f32[1,1,4096]{2,1,0:T(1,128)}, u32[]{:S(2)}) copy-start(f32[1,1,4096]{2,1,0:T(1,128)} %param.17) | copy-start | bytes 49156

commit v3 on v2

--- a/solution.py
+++ b/solution.py
@@ -15,6 +15,7 @@
 LANES = 128
 SUB = 8
 EDGE = 4
+GROUP = 2
 
 
 gravity = 9.81
@@ -36,18 +37,14 @@
     root = jnp.exp2(POWER * jnp.log(floored))
     drag = (gravity * time_step * friction) * jnp.abs(flow) * root
     pushed = flow - (gravity * time_step) * face_depth * (eta_next - eta)
-    return pushed / (1.0 + drag)
-
-
-def steps_kernel(cs, row0, rows, kind, group, *refs):
-    depth, ground, frow, fcol, top, bottom, side, wet, shift = refs[:9]
-    if kind == "all":
-        outs, scratch = refs[9:12], refs[12:]
-    else:
-        if kind == "rows":
-            refs = refs[:9] + refs[10:]
-        outs, scratch = refs[9:10], refs[10:]
-    d, g, f, c, w8, zc, zero, in_sem, out_sem = scratch
+    return pushed * pl.reciprocal(1.0 + drag)
+
+
+def steps_kernel(cs, rows, group, *refs):
+    row0 = 0
+    depth, ground, frow, fcol, top, bottom, side, wet, shift_rows, shift_cols = refs[:10]
+    outs, edge_rows, edge_cols = refs[10:13], refs[13], refs[14]
+    d, g, f, c, w8, zc, zero, in_sem, out_sem, row_sem, col_sem = refs[15:]
     n = len(cs)
     high = rows - row0 + 32
     arrays = ((depth, d), (ground, g), (frow, f), (fcol, c))
@@ -71,8 +68,7 @@
     for a, dst in enumerate((d, g, f, c, w8)):
         base = (n - 1) * high if a < 4 else 0
         dst[pl.ds(base, high), :] = pltpu.roll(mixed, LANES - 8 * a - EDGE, 1)
-    if kind != "all":
-        zero[...] = jnp.zeros_like(zero)
+    zero[...] = jnp.zeros_like(zero)
     for copy in copies:
         copy.wait()
 
@@ -145,66 +141,54 @@
         block(last, 1, bottom_active, carry)
 
     span = MAX_BLOCKS * BLOCK
-    state = (d, f, c)
     copies = []
-    for a, src in enumerate(state):
-        if kind == "all":
-            for i, slab in enumerate(cs[:-1]):
-                copies.append(pltpu.make_async_copy(
-                    src.at[pl.ds(i * high + 16, rows)], outs[a].at[:, pl.ds(slab * LANES, LANES)], out_sem.at[a, i]))
-                copies[-1].start()
-            continue
+
+    def hand_on(src, dst, sem, keep):
+        copy = pltpu.make_async_copy(src, dst, sem)
+        hole = pltpu.make_async_copy(zero.at[pl.ds(0, src.shape[0])], dst, sem)
+        pl.when(keep)(copy.start)
+        pl.when(jnp.logical_not(keep))(hole.start)
+        copies.append(copy)
+
+    for a, src in enumerate((d, f, c)):
+        for i, slab in enumerate(cs[:-1]):
+            lanes = pl.ds(slab * LANES, LANES)
+            copies.append(pltpu.make_async_copy(
+                src.at[pl.ds(i * high + 16, rows)], outs[a].at[:, lanes], out_sem.at[a, i]))
+            copies[-1].start()
+            for k in range(MAX_BLOCKS):
+                hand_on(src.at[pl.ds(i * high + high - 16 - span + k * BLOCK, BLOCK)],
+                        edge_rows.at[a, pl.ds(k * BLOCK, BLOCK), lanes], row_sem.at[a, k, i],
+                        k >= MAX_BLOCKS - shift_rows[0, 0])
         for k in range(MAX_BLOCKS):
-            keep = k >= MAX_BLOCKS - shift[0, 0]
-            if kind == "cols":
-                pieces = [(src.at[pl.ds((n - 1 - MAX_BLOCKS + k) * high + 16, rows)], zero,
-                           outs[0].at[a, :, pl.ds(k * BLOCK, BLOCK)], k)]
-            else:
-                pieces = [(src.at[pl.ds(i * high + high - 16 - span + k * BLOCK, BLOCK)], zero,
-                           outs[0].at[a, pl.ds(k * BLOCK, BLOCK), pl.ds(slab * LANES, LANES)], k * n + i)
-                          for i, slab in enumerate(cs[:-1])]
-            for data, empty, dst, m in pieces:
-                copy = pltpu.make_async_copy(data, dst, out_sem.at[a, m])
-                hole = pltpu.make_async_copy(empty, dst, out_sem.at[a, m])
-                pl.when(keep)(copy.start)
-                pl.when(jnp.logical_not(keep))(hole.start)
-                copies.append(copy)
+            hand_on(src.at[pl.ds((n - 1 - MAX_BLOCKS + k) * high + 16, rows)],
+                    edge_cols.at[a, :, pl.ds(k * BLOCK, BLOCK)], col_sem.at[a, k],
+                    k >= MAX_BLOCKS - shift_cols[0, 0])
     for copy in copies:
         copy.wait()
 
 
-def steps_call(kind, args):
+def steps_call(*args):
     rows, width = args[0].shape
-    slabs = width // LANES
-    cs, row0, group = list(range(slabs + 1)), 0, 2
     span = MAX_BLOCKS * BLOCK
-    if kind == "cols":
-        cs, group = cs[slabs - MAX_BLOCKS - 1:], 4
-        out = [jax.ShapeDtypeStruct((3, rows, span), jnp.float32)]
-        zero, sems = (rows, LANES), MAX_BLOCKS
-    elif kind == "rows":
-        row0 = rows - span - 2 * SUB
-        out = [jax.ShapeDtypeStruct((3, span, width), jnp.float32)]
-        zero, sems = (BLOCK, LANES), MAX_BLOCKS * len(cs)
-    else:
-        out = [jax.ShapeDtypeStruct((rows, width), jnp.float32)] * 3
-        zero, sems = (SUB, LANES), len(cs)
-    n, high = len(cs), rows - row0 + 32
+    cs = list(range(width // LANES + 1))
+    n, high = len(cs), rows + 32
     anywhere = pl.BlockSpec(memory_space=pltpu.HBM)
     vmem = pl.BlockSpec(memory_space=pltpu.VMEM)
     smem = pl.BlockSpec(memory_space=pltpu.SMEM)
+    shapes = [(rows, width)] * 3 + [(3, span, width), (3, rows, span)]
     buffer = pltpu.VMEM((n * high, LANES), jnp.float32)
-    cells = n * high * LANES
     return pl.pallas_call(
-        functools.partial(steps_kernel, cs, row0, rows, kind, group),
-        out_shape=out,
-        in_specs=[anywhere] * 4 + [vmem, vmem, vmem, smem, smem] + [anywhere] * (kind == "rows"),
-        out_specs=[anywhere] * len(out),
-        scratch_shapes=[buffer] * 4 + [pltpu.VMEM((high, LANES), jnp.float32), buffer, pltpu.VMEM(zero, jnp.float32),
-                                       pltpu.SemaphoreType.DMA((4, n)), pltpu.SemaphoreType.DMA((3, sems))],
+        functools.partial(steps_kernel, cs, rows, GROUP),
+        out_shape=[jax.ShapeDtypeStruct(shape, jnp.float32) for shape in shapes],
+        in_specs=[anywhere] * 4 + [vmem] * 3 + [smem] * 3,
+        out_specs=[anywhere] * len(shapes),
+        scratch_shapes=[buffer] * 4 + [pltpu.VMEM((high, LANES), jnp.float32), buffer,
+                                       pltpu.VMEM((rows, LANES), jnp.float32), pltpu.SemaphoreType.DMA((4, n)),
+                                       pltpu.SemaphoreType.DMA((3, n)), pltpu.SemaphoreType.DMA((3, MAX_BLOCKS, n)),
+                                       pltpu.SemaphoreType.DMA((3, MAX_BLOCKS))],
         compiler_params=pltpu.CompilerParams(vmem_limit_bytes=58 << 20),
-        cost_estimate=pl.CostEstimate(flops=cells, transcendentals=0, bytes_accessed=cells),
-        name="steps_" + kind,
+        name="steps",
     )(*args)
 
 
@@ -237,7 +221,7 @@
         scratch_shapes=[pltpu.VMEM((rows * width // LANES, LANES), jnp.float32),
                         pltpu.SemaphoreType.DMA((width // LANES,))],
         compiler_params=pltpu.CompilerParams(vmem_limit_bytes=58 << 20),
-        cost_estimate=pl.CostEstimate(flops=0, transcendentals=0, bytes_accessed=8 * rows * width),
+        cost_estimate=pl.CostEstimate(flops=0, transcendentals=0, bytes_accessed=rows * width),
         name="pick_rows",
     )(spots, depth)
 
@@ -399,12 +383,10 @@
     tile_rows, tile_cols = depth.shape
     arrays = (depth, ground, flow_rows, flow_cols)
     top, bottom, side = halos(arrays, wet_tiles)
-    common = arrays + (top, bottom, side, wet_tiles)
-    (edge_cols,) = steps_call("cols", common + (shift_cols,))
+    depth, flow_rows, flow_cols, edge_rows, edge_cols = steps_call(
+        *arrays, top, bottom, side, wet_tiles, shift_rows, shift_cols)
     moved_cols = passed_along(edge_cols, "col", 1)
-    (edge_rows,) = steps_call("rows", common + (shift_rows, edge_cols))
     moved_rows = passed_along(edge_rows, "row", 1)
-    depth, flow_rows, flow_cols = steps_call("all", common + (shift_rows,))
     devices = lax.axis_size("row") * lax.axis_size("col")
     cells = inlet_cell[0, 0]
     cell_row, cell_col = cells // tile_cols, cells % tile_cols

time: 149 us -> 132 us (0.89)
  the two profiles are of different devices: /device:TPU:0 before, /device:TPU:17 now
where the time goes in v3:
time: 132 us; the launch traced here: 131 us
  Pallas kernels  114 us (86%)
  starting transfers between devices  5.52 us (4%)
  local copies, waits for them, and re-layouts  4.19 us (3%)
  other arithmetic  3.16 us (2%)
  between operations  2.68 us (2%)
  matrix products  1.85 us (1%)
    pallas_call x1, Pallas kernels, steps_call(): pl.pallas_call(functools.partial(steps_kernel, cs, rows, GROUP), out_shap...  50.6 us
    pallas_call x1, Pallas kernels, to_owners(): pl.pallas_call(functools.partial(owners_kernel, counts), out_shape=jax.Sh...  41.5 us
    pallas_call x1, Pallas kernels, halos(): pl.pallas_call(functools.partial(halo_kernel, counts), out_shape=[jax.Sha...  13 us
    pallas_call x1, Pallas kernels, pick_rows(): pl.pallas_call(pick_kernel, out_shape=jax.ShapeDtypeStruct((count, LANES)...  8.78 us
    ppermute x2, starting transfers between devices, passed_along(): lax.ppermute(value, axis, [(source, source + steps) for source in range(l...  5.52 us
    unnamed x8, local copies, waits for them, and re-layouts  3.08 us
  transfers between devices with their start and end apart: 2, of which 0 were waited for; matrix products, arithmetic and copies ran while one was open for 5% of the time, Pallas kernels for 38%

profile of v3, /device:TPU:17, one launch (start us, length us, event | category | flops | bytes accessed | tf_op | source)
XLA Modules:
  0.0 131.3 jit_solution(2641686819832386422)
XLA Ops:
  2.6 13.0 %halos.1 = (f32[40,1024]{1,0:T(8,128)}, f32[40,1024]{1,0:T(8,128)}, f32[1024,128]{1,0:T(8,128)}) custom-call(f32[768,1024]{1,0:T(8,128)} %refs_0_.1, f32[768,1024]{1,0:T(8,128)} %refs_1_.1, f32[768,1024]{1,0:T(8,128)} %refs_2_.1, f32[768,1024]{1,0:T(8,128)} %refs_3_.1, s32[1,1]{1,0:T(1,128)S(6)} %copy.18.wet.refs_7_), custom_call_target="tpu_custom_call" | custom-call | tf_op jit(solution)/shard_map/halos/pallas_call | solution.py:310
  15.6 0.0 copy-start
  15.6 50.6 %steps.1 = (f32[768,1024]{1,0:T(8,128)}, f32[768,1024]{1,0:T(8,128)}, f32[768,1024]{1,0:T(8,128)}, f32[3,256,1024]{2,1,0:T(8,128)}, f32[3,768,256]{2,1,0:T(8,128)}) custom-call(f32[768,1024]{1,0:T(8,128)} %refs_0_.1, f32[768,1024]{1,0:T(8,128)} %refs_1_.1, f32[768,1024]{1,0:T(8,128)} %refs_2_.1, f32[768,1024]{1,0:T(8,128)} %refs_3_.1, ...), custom_call_target="tpu_custom_call" | custom-call | tf_op jit(solution)/shard_map/steps/pallas_call | solution.py:181
  66.2 3.4 %collective-permute-start = (f32[3,256,1024]{2,1,0:T(8,128)}, f32[3,256,1024]{2,1,0:T(8,128)S(1)}, u32[]{:S(2)}, u32[]{:S(2)}) collective-permute-start(f32[3,256,1024]{2,1,0:T(8,128)} %get-tuple-element.20), channel_id=1, source_target_pairs={{0,8},{8,16},{16,24},{1,9},{9,17},{17,25},{2,10},{10,18},{18,26},{... | collective-permute-start | bytes 9437192 | tf_op jit(solution)/shard_map/ppermute | solution.py:31
  69.6 2.1 %collective-permute-start.1 = (f32[3,768,256]{2,1,0:T(8,128)}, f32[3,768,256]{2,1,0:T(8,128)S(1)}, u32[]{:S(2)}, u32[]{:S(2)}) collective-permute-start(f32[3,768,256]{2,1,0:T(8,128)} %get-tuple-element.21), channel_id=1, source_target_pairs={{0,1},{1,2},{2,3},{3,4},{4,5},{5,6},{6,7},{8,9},{9,10},{10,11},{11... | collective-permute-start | bytes 7077896 | tf_op jit(solution)/shard_map/ppermute | solution.py:31
  71.8 0.0 copy-done
  71.8 0.6 add_select_fusion.3
  72.4 0.0 copy-start.1
  72.4 0.0 copy-start.2
  72.4 8.8 %pick_rows.1 = f32[4096,128]{1,0:T(8,128)} custom-call(s32[4096]{0:T(1024)} %get-tuple-element.25.spots, f32[768,1024]{1,0:T(8,128)} %get-tuple-element.32.depth), custom_call_target="tpu_custom_call" | custom-call | bytes 786432 | tf_op jit(solution)/shard_map/pick_rows/pallas_call | solution.py:216
  81.2 2.5 %select_reduce_fusion = f32[4096]{0:T(1024)S(1)} fusion(f32[4096,128]{1,0:T(8,128)} %pick_rows.1, s32[4096]{0:T(1024)S(1)} %get-tuple-element.24), kind=kLoop, calls=%fused_computation.1 | loop fusion | flops 1568768 | bytes 2129920 | tf_op jit(solution)/shard_map/reduce_sum | solution.py:395
  83.7 0.0 copy-done.1
  83.7 0.0 copy-done.2
  83.8 1.9 %fusion = f32[32,128]{1,0:T(8,128)} fusion(s32[4096]{0:T(1024)S(1)} %get-tuple-element.23, f32[4096]{0:T(1024)S(1)} %maximum_multiply_fusion, s32[4096]{0:T(1024)S(1)} %get-tuple-element.22), kind=kOutput, calls=%fused_computation.3 | convolution fusion | flops 202113024 | bytes 65536 | tf_op jit(solution)/shard_map/dot_general | solution.py:400
  85.6 41.5 %to_owners.1 = f32[1,128]{1,0:T(1,128)} custom-call(f32[32,1,128]{2,1,0:T(1,128)} %bitcast.9), custom_call_target="tpu_custom_call" | custom-call | tf_op jit(solution)/shard_map/to_owners/pallas_call | solution.py:359
  127.1 1.1 slice_bitcast_fusion
  128.2 0.0 collective-permute-done.1
  128.2 0.0 collective-permute-done
  128.2 1.7 %copy.21 = f32[3,256,1024]{2,1,0:T(8,128)} copy(f32[3,256,1024]{2,1,0:T(8,128)S(1)} %collective-permute-done) | data formatting | bytes 6291456
  129.9 1.4 %copy.22 = f32[3,768,256]{2,1,0:T(8,128)} copy(f32[3,768,256]{2,1,0:T(8,128)S(1)} %collective-permute-done.1) | data formatting | bytes 4718592
  (2 shorter events, 0.0 us)
Async XLA Ops:
  15.6 56.2 %copy-start = (s32[1,1,4096]{2,1,0:T(1,128)S(1)}, s32[1,1,4096]{2,1,0:T(1,128)}, u32[]{:S(2)}) copy-start(s32[1,1,4096]{2,1,0:T(1,128)} %param.15) | copy-start | bytes 49156
  66.2 62.0 %collective-permute-start = (f32[3,256,1024]{2,1,0:T(8,128)}, f32[3,256,1024]{2,1,0:T(8,128)S(1)}, u32[]{:S(2)}, u32[]{:S(2)}) collective-permute-start(f32[3,256,1024]{2,1,0:T(8,128)} %get-tuple-element.20), channel_id=1, source_target_pairs={{0,8},{8,16},{16,24},{1,9},{9,17},{17,25},{2,10},{10,18},{18,26},{... | collective-permute-start | bytes 9437192 | tf_op jit(solution)/shard_map/ppermute | solution.py:31
  69.6 58.6 %collective-permute-start.1 = (f32[3,768,256]{2,1,0:T(8,128)}, f32[3,768,256]{2,1,0:T(8,128)S(1)}, u32[]{:S(2)}, u32[]{:S(2)}) collective-permute-start(f32[3,768,256]{2,1,0:T(8,128)} %get-tuple-element.21), channel_id=1, source_target_pairs={{0,1},{1,2},{2,3},{3,4},{4,5},{5,6},{6,7},{8,9},{9,10},{10,11},{11... | collective-permute-start | bytes 7077896 | tf_op jit(solution)/shard_map/ppermute | solution.py:31
  72.4 11.3 %copy-start.1 = (s32[1,1,4096]{2,1,0:T(1,128)S(1)}, s32[1,1,4096]{2,1,0:T(1,128)}, u32[]{:S(2)}) copy-start(s32[1,1,4096]{2,1,0:T(1,128)} %param.16) | copy-start | bytes 49156
  72.4 11.3 %copy-start.2 = (f32[1,1,4096]{2,1,0:T(1,128)S(1)}, f32[1,1,4096]{2,1,0:T(1,128)}, u32[]{:S(2)}) copy-start(f32[1,1,4096]{2,1,0:T(1,128)} %param.17) | copy-start | bytes 49156
